TPU v7x, 32 devices: a whole 2x2x4 slice. The times are simulated.
32 devices in a mesh: head: 8 (over z, y), fsdp: 4 (over x, core).
Axes of the slice: x: 2, y: 2, z: 4, core: 2. Of those that a mesh axis runs over, the one named last changes fastest.
Arguments:
- hidden: bfloat16 [4, 1024, 2048], P('fsdp', 'head'), may hold values from -6 to 6
- w_qkv: bfloat16 [2048, 6144], P(('head', 'fsdp')), may hold values from -0.125 to 0.125
- w_out: bfloat16 [2048, 2048], P(('head', 'fsdp')), may hold values from -0.75 to 0.75
- w_router: bfloat16 [2048, 16], P(('head', 'fsdp')), may hold values from -0.0625 to 0.0625
- g_attn: bfloat16 [2048], P(('head', 'fsdp')), may hold values from 0.099609375 to 1.8984375
- g_ffn: bfloat16 [2048], P(('head', 'fsdp')), may hold values from 0.099609375 to 1.8984375
- g_q: bfloat16 [2048], P(('head', 'fsdp')), may hold values from 0.69921875 to 2
- g_k: bfloat16 [2048], P(('head', 'fsdp')), may hold values from 0.69921875 to 2
- w_gate: bfloat16 [16, 2048, 1024], P('head', 'fsdp'), may hold values from -0.125 to 0.125
- w_up: bfloat16 [16, 2048, 1024], P('head', 'fsdp'), may hold values from -0.125 to 0.125
- w_down: bfloat16 [16, 1024, 2048], P('head', 'fsdp'), may hold values from -0.75 to 0.75
- lengths: int32 [4], P('fsdp'), may hold values from 256 to 1024, as said below
- routes: int32 [4, 1024, 8], P('fsdp', 'head'), may hold values from 0 to 15, all different within a row; in each aligned block of 128 rows (0 to 127, 128 to 255, ..., all dimensions but the last counted through in order) at most 96 rows name the same one
- route_codes: int32 [4, 1024, 8], P('fsdp', 'head'), may hold values from -384 to 383
- cotangent: bfloat16 [4, 1024, 2048], P('fsdp', 'head'), may hold values from -6 to 6
Outputs:
- out: bfloat16 [4, 1024, 2048], P('fsdp', 'head')
- d_hidden: float32 [4, 1024, 2048], P('fsdp', 'head')
- d_w_qkv: float32 [2048, 6144], P(('head', 'fsdp'))
- d_w_out: float32 [2048, 2048], P(('head', 'fsdp'))
- d_w_router: float32 [2048, 16], P(('head', 'fsdp'))
- d_g_attn: float32 [2048], P(('head', 'fsdp'))
- d_g_ffn: float32 [2048], P(('head', 'fsdp'))
- d_g_q: float32 [2048], P(('head', 'fsdp'))
- d_g_k: float32 [2048], P(('head', 'fsdp'))
- d_w_gate: float32 [16, 2048, 1024], P('head', 'fsdp')
- d_w_up: float32 [16, 2048, 1024], P('head', 'fsdp')
- d_w_down: float32 [16, 1024, 2048], P('head', 'fsdp')
Inputs may be any that keep to these rules, and one draw needn't show every extreme that they name: `lengths`: keys at positions at or after a sequence's length are masked. Some sequence has 1024 valid slots, some 1024 // 4. Each token names 8 different experts. In the 128 tokens of one device no expert is named by more than 96 routes, and some expert reaches 96.
All inputs are finite; a program needn't handle non-finite values.
Results may differ from a plain program's by a relative error of at most 0.018.
Values may be sent and summed in bfloat16 or wider, within the bound.
A program may use at most 256 MiB of HBM per device.

v0:
```python
import math
import jax
import jax.numpy as jnp
from jax import lax
from jax.sharding import PartitionSpec as P

HEADS = 16
HD = 128
FF = 1024
TOP = 8
EXP_DEV = 2
EPS = 1e-06
ROPE_BASE = 10000.0
NEGATIVE = -1e30
BF = jnp.bfloat16
F32 = jnp.float32


def ring_head(n, k):
    k %= n
    return 2 * k if k < n // 2 else 2 * n - 1 - 2 * k


def ring_links(n):
    right = [(ring_head(n, k), ring_head(n, k + 1)) for k in range(n)]
    return (right, [(b, a) for a, b in right])


def ring_place():
    n = lax.axis_size("head")
    me = lax.axis_index("head")
    odd = me % 2
    return (1 - odd) * (me // 2) + odd * (n - 1 - me // 2)


def head_at(offset):
    n = lax.axis_size("head")
    k = (ring_place() + offset + n) % n
    down = k // (n // 2)
    return (1 - down) * 2 * k + down * (2 * n - 1 - 2 * k)


def gather_ring(block):
    n = lax.axis_size("head")
    right, left = ring_links(n)
    half = n // 2
    rows = block.shape[0] // 2
    out = jnp.zeros((n,) + block.shape, block.dtype)

    def put(out, piece, offset):
        return lax.dynamic_update_slice_in_dim(out, piece[None], head_at(offset), 0)

    out = put(out, block, 0)
    r = l = block
    for step in range(1, half):
        r = lax.ppermute(r, "head", right)
        l = lax.ppermute(l, "head", left)
        out = put(out, r, -step)
        out = put(out, l, step)
    a = lax.ppermute(r[:rows], "head", right)
    b = lax.ppermute(l[rows:], "head", left)
    return put(out, jnp.concatenate([a, b], 0), half)


def scatter_ring(parts):
    n = lax.axis_size("head")
    right, left = ring_links(n)
    half = n // 2
    rows = parts.shape[1] // 2

    def piece(offset):
        return lax.dynamic_index_in_dim(parts, head_at(offset), 0, keepdims=False)

    far = piece(half)
    r = lax.ppermute(far[:rows], "head", right)
    l = lax.ppermute(far[rows:], "head", left)
    for step in range(half - 1, 0, -1):
        br = piece(step).astype(F32)
        bl = piece(-step).astype(F32)
        if step == half - 1:
            br = jnp.concatenate([br[:rows] + r.astype(F32), br[rows:]], 0)
            bl = jnp.concatenate([bl[:rows], bl[rows:] + l.astype(F32)], 0)
        else:
            br = br + r.astype(F32)
            bl = bl + l.astype(F32)
        r = lax.ppermute(br.astype(BF), "head", right)
        l = lax.ppermute(bl.astype(BF), "head", left)
    return piece(0).astype(F32) + r.astype(F32) + l.astype(F32)


def rotate(values, cosine, sine):
    half = HD // 2
    shaped = values.reshape(values.shape[0], -1, HD)
    first = shaped[..., :half]
    second = shaped[..., half:]
    turned = jnp.concatenate(
        [first * cosine - second * sine, second * cosine + first * sine], axis=-1
    )
    return turned.reshape(values.shape)


def dot(a, b, dims=((1,), (0,))):
    return lax.dot_general(a, b, (dims, ((), ())), preferred_element_type=F32)


NT = ((1,), (1,))
TN = ((0,), (0,))


def body(
    hidden,
    w_qkv,
    w_out,
    w_router,
    g_attn,
    g_ffn,
    g_q,
    g_k,
    w_gate,
    w_up,
    w_down,
    lengths,
    routes,
    route_codes,
    cotangent,
):
    n = lax.axis_size("head")
    m = lax.axis_size("fsdp")
    me = lax.axis_index("head")
    rows = hidden.shape[1]
    width = hidden.shape[2]
    seq = rows * n
    lh = HEADS // n
    dh = lh * HD
    experts = EXP_DEV * n
    shard = w_qkv.shape[0]
    scale = 1.0 / math.sqrt(HD)
    both = ("head", "fsdp")
    small = jnp.concatenate(
        [w_router, g_attn[:, None], g_ffn[:, None], g_q[:, None], g_k[:, None]], axis=1
    )
    small = lax.all_gather(small, both, axis=0, tiled=True)
    router = small[:, :experts]
    gain_attn = small[:, experts].astype(F32)
    gain_ffn = small[:, experts + 1].astype(F32)
    gains_q = lax.dynamic_slice_in_dim(small[:, experts + 2], me * dh, dh, 0).astype(F32)
    gains_k = lax.dynamic_slice_in_dim(small[:, experts + 3], me * dh, dh, 0).astype(F32)
    cols = w_qkv.reshape(shard, 3, n, dh).transpose(2, 0, 1, 3).reshape(n, shard, 3 * dh)
    cols = lax.all_to_all(cols, "head", split_axis=0, concat_axis=0, tiled=True)
    qkv = lax.all_gather(cols, "fsdp", axis=1, tiled=True).reshape(width, 3 * dh)
    tokens_all = gather_ring(hidden[0]).reshape(seq, width)
    info = gather_ring(jnp.concatenate([routes[0], route_codes[0]], axis=1)).reshape(seq, 2 * TOP)
    full_out = lax.all_gather(w_out, both, axis=0, tiled=True)
    full_gate = lax.all_gather(w_gate, "fsdp", axis=1, tiled=True)
    full_up = lax.all_gather(w_up, "fsdp", axis=1, tiled=True)
    full_down = lax.all_gather(w_down, "fsdp", axis=1, tiled=True)

    def own(values):
        return lax.dynamic_slice_in_dim(values, me * rows, rows, 0)

    def inverse_rms(values):
        return lax.rsqrt(jnp.mean(values * values, axis=-1, keepdims=True) + EPS)

    wide = tokens_all.astype(F32)
    attn_input = (wide * inverse_rms(wide) * gain_attn).astype(BF)
    projected = dot(attn_input, qkv)
    proj_q = projected[:, :dh]
    proj_k = projected[:, dh : 2 * dh]
    squares = jnp.stack([jnp.sum(proj_q * proj_q, axis=1), jnp.sum(proj_k * proj_k, axis=1)])
    squares = lax.psum(squares, "head") / width
    inv_q = lax.rsqrt(squares[0] + EPS)[:, None]
    inv_k = lax.rsqrt(squares[1] + EPS)[:, None]
    frequency = ROPE_BASE ** (-2.0 * jnp.arange(HD // 2, dtype=F32) / HD)
    angles = jnp.arange(seq, dtype=F32)[:, None] * frequency[None, :]
    cosine = jnp.cos(angles)[:, None, :]
    sine = jnp.sin(angles)[:, None, :]
    queries = rotate(proj_q * inv_q * gains_q, cosine, sine).astype(BF)
    keys = rotate(proj_k * inv_k * gains_k, cosine, sine).astype(BF)
    values = projected[:, 2 * dh :].astype(BF)
    valid = jnp.arange(seq, dtype=jnp.int32) < lengths[0]

    def probs_of(q, k):
        scores = jnp.where(valid[None, :], dot(q, k, NT) * scale, NEGATIVE)
        exponent = jnp.exp(scores - jnp.max(scores, axis=-1, keepdims=True))
        return exponent / jnp.sum(exponent, axis=-1, keepdims=True)

    attended = []
    for head in range(lh):
        part = slice(head * HD, (head + 1) * HD)
        probabilities = probs_of(queries[:, part], keys[:, part]).astype(BF)
        attended.append(dot(probabilities, values[:, part]).astype(BF))
    attended = jnp.concatenate(attended, axis=1)
    attended_all = gather_ring(attended).transpose(1, 0, 2).reshape(seq, width)
    residual = wide + dot(attended_all, full_out)
    inv_ffn = inverse_rms(residual)
    ffn_input = (residual * inv_ffn * gain_ffn).astype(BF)
    logits = dot(ffn_input, router)
    matches = info[:, :TOP, None] == jnp.arange(experts, dtype=jnp.int32)[None, None, :]
    chosen = (
        jnp.sum(jnp.where(matches, logits[:, None, :], 0.0), axis=-1)
        + info[:, TOP:].astype(F32) / 1024.0
    )
    chosen = jnp.exp(chosen - jnp.max(chosen, axis=1, keepdims=True))
    gates = chosen / jnp.sum(chosen, axis=1, keepdims=True)
    spread = jnp.sum(jnp.where(matches, gates[:, :, None], 0.0), axis=1)
    mine = lax.dynamic_slice_in_dim(spread, me * EXP_DEV, EXP_DEV, 1)
    cot_all = gather_ring(cotangent[0]).reshape(seq, width)
    mixed = jnp.zeros((seq, width), F32)
    grad_in = jnp.zeros((seq, width), F32)
    gate_dots, gate_grads, up_grads, down_grads = ([], [], [], [])
    for e in range(EXP_DEV):
        gate = mine[:, e : e + 1]
        gate_pre = dot(ffn_input, full_gate[e])
        up_pre = dot(ffn_input, full_up[e])
        sig = jax.nn.sigmoid(gate_pre)
        silu = gate_pre * sig
        act = (silu * up_pre).astype(BF)
        produced = dot(act, full_down[e]).astype(BF).astype(F32)
        mixed = mixed + gate * produced
        cot_f = cot_all.astype(F32)
        gate_dots.append(jnp.sum(produced * cot_f, axis=1))
        grad_out = (gate * cot_f).astype(BF)
        grad_act = dot(grad_out, full_down[e], NT)
        grad_gate_pre = (grad_act * up_pre * sig * (1.0 + gate_pre * (1.0 - sig))).astype(BF)
        grad_up_pre = (grad_act * silu).astype(BF)
        down_grads.append(dot(act, grad_out, TN).astype(BF))
        gate_grads.append(dot(ffn_input, grad_gate_pre, TN).astype(BF))
        up_grads.append(dot(ffn_input, grad_up_pre, TN).astype(BF))
        grad_in = grad_in + dot(grad_gate_pre, full_gate[e], NT) + dot(grad_up_pre, full_up[e], NT)
    grad_ffn = scatter_ring(grad_in.astype(BF).reshape(n, rows, width))
    summed = scatter_ring(mixed.astype(BF).reshape(n, rows, width))

    def over_fsdp(grads):
        return lax.psum_scatter(jnp.stack(grads), "fsdp", scatter_dimension=1, tiled=True).astype(
            F32
        )

    grad_w_gate = over_fsdp(gate_grads)
    grad_w_up = over_fsdp(up_grads)
    grad_w_down = over_fsdp(down_grads)
    dots = jnp.stack(gate_dots).reshape(EXP_DEV, n, rows).transpose(1, 0, 2)
    dots = lax.all_to_all(dots, "head", split_axis=0, concat_axis=0, tiled=True)
    dots = dots.reshape(experts, rows).T
    own_spread = own(spread)
    own_residual = own(residual)
    out_rows = own_residual + summed
    grad_rows = cotangent[0].astype(F32)
    grad_logits = own_spread * (dots - jnp.sum(own_spread * dots, axis=1, keepdims=True))
    high = lax.Precision.HIGHEST
    grad_ffn = grad_ffn + jnp.dot(grad_logits, router.astype(F32).T, precision=high)
    grad_router = jnp.dot(own(ffn_input).astype(F32).T, grad_logits, precision=high)

    def norm_back(values, gain, grad):
        inv = inverse_rms(values)
        unit = values * inv
        scaled = grad * gain
        back = inv * (scaled - unit * jnp.mean(scaled * unit, axis=-1, keepdims=True))
        return (back, jnp.sum(grad * unit, axis=0))

    back, grad_gain_ffn = norm_back(own_residual, gain_ffn, grad_ffn)
    grad_residual = grad_rows + back
    grad_attn_out = grad_residual.astype(BF)
    grad_attended = dot(grad_attn_out, full_out, NT).astype(BF)
    grad_heads = lax.all_to_all(
        grad_attended.reshape(rows, n, dh), "head", split_axis=1, concat_axis=0, tiled=True
    ).reshape(seq, dh)
    grad_q, grad_k, grad_v = ([], [], [])
    for head in range(lh):
        part = slice(head * HD, (head + 1) * HD)
        probabilities = probs_of(queries[:, part], keys[:, part])
        grad_probs = dot(grad_heads[:, part], values[:, part], NT)
        inner = jnp.sum(probabilities * grad_probs, axis=-1, keepdims=True)
        grad_scores = (probabilities * (grad_probs - inner)).astype(BF)
        grad_q.append((dot(grad_scores, keys[:, part]) * scale).astype(BF))
        grad_k.append((dot(grad_scores, queries[:, part], TN) * scale).astype(BF))
        grad_v.append(dot(probabilities.astype(BF), grad_heads[:, part], TN).astype(BF))
    turned_q = rotate(jnp.concatenate(grad_q, axis=1).astype(F32), cosine, -sine)
    turned_k = rotate(jnp.concatenate(grad_k, axis=1).astype(F32), cosine, -sine)
    unit_q = proj_q * inv_q
    unit_k = proj_k * inv_k
    means = jnp.stack(
        [jnp.sum(turned_q * gains_q * unit_q, axis=1), jnp.sum(turned_k * gains_k * unit_k, axis=1)]
    )
    means = lax.psum(means, "head") / width
    grad_projected = jnp.concatenate(
        [
            (inv_q * (turned_q * gains_q - unit_q * means[0][:, None])).astype(BF),
            (inv_k * (turned_k * gains_k - unit_k * means[1][:, None])).astype(BF),
            jnp.concatenate(grad_v, axis=1),
        ],
        axis=1,
    )
    grad_gain_q = jnp.sum(turned_q * unit_q, axis=0)
    grad_gain_k = jnp.sum(turned_k * unit_k, axis=0)
    grad_attn_in = dot(grad_projected, qkv, NT).astype(BF)
    grad_attn_in = scatter_ring(grad_attn_in.reshape(n, rows, width))
    grad_qkv = dot(attn_input, grad_projected, TN).astype(BF).reshape(n, m * shard, 3 * dh)
    grad_qkv = lax.psum_scatter(grad_qkv, "fsdp", scatter_dimension=1, tiled=True)
    grad_qkv = lax.all_to_all(grad_qkv, "head", split_axis=0, concat_axis=0, tiled=True)
    grad_qkv = grad_qkv.reshape(n, shard, 3, dh).transpose(1, 2, 0, 3).reshape(shard, 3 * width)
    grad_all = gather_ring(grad_attn_out).reshape(seq, width)
    grad_out_w = dot(attended, grad_all, TN)
    grad_out_w = lax.psum_scatter(grad_out_w, "fsdp", scatter_dimension=0, tiled=True)
    back, grad_gain_attn = norm_back(hidden[0].astype(F32), gain_attn, grad_attn_in)
    grad_hidden = grad_residual + back

    def at_mine(piece):
        return lax.dynamic_update_slice_in_dim(jnp.zeros((width,), F32), piece, me * dh, 0)[:, None]

    pack = jnp.concatenate(
        [
            grad_router,
            grad_gain_attn[:, None],
            grad_gain_ffn[:, None],
            at_mine(grad_gain_q),
            at_mine(grad_gain_k),
        ],
        axis=1,
    ).reshape(n * m, shard * (experts + 4))
    pack = lax.all_to_all(pack, both, split_axis=0, concat_axis=0, tiled=True)
    pack = jnp.sum(pack, axis=0).reshape(shard, experts + 4)
    return (
        out_rows.astype(BF)[None],
        grad_hidden[None],
        grad_qkv.astype(F32),
        grad_out_w,
        pack[:, :experts],
        pack[:, experts],
        pack[:, experts + 1],
        pack[:, experts + 2],
        pack[:, experts + 3],
        grad_w_gate,
        grad_w_up,
        grad_w_down,
    )


def solution(mesh):
    both = ("head", "fsdp")
    return jax.shard_map(
        body,
        mesh=mesh,
        in_specs=(
            P("fsdp", "head", None),
            P(both, None),
            P(both, None),
            P(both, None),
            P(both),
            P(both),
            P(both),
            P(both),
            P("head", "fsdp", None),
            P("head", "fsdp", None),
            P("head", "fsdp", None),
            P("fsdp"),
            P("fsdp", "head", None),
            P("fsdp", "head", None),
            P("fsdp", "head", None),
        ),
        out_specs=(
            P("fsdp", "head", None),
            P("fsdp", "head", None),
            P(both, None),
            P(both, None),
            P(both, None),
            P(both),
            P(both),
            P(both),
            P(both),
            P("head", "fsdp", None),
            P("head", "fsdp", None),
            P("head", "fsdp", None),
        ),
        check_vma=False,
    )
```

profile of v0, /device:TPU:0, one launch (start us, length us, event | category | flops | bytes accessed | tf_op | source)
XLA Modules:
  0.0 871.2 jit_solution(12422500406623019625)
XLA Ops:
  10.0 27.5 %all_to_all.40 = bf16[8,64,768]{2,1,0:T(8,128)(2,1)} all-to-all(bf16[8,64,768]{2,1,0:T(8,128)(2,1)S(1)} %reshape.375), channel_id=1, replica_groups=mesh['head'=8,'fsdp'=4] {'head'}, dimensions={0} | all-to-all | bytes 1572864 | tf_op jit(solution)/shard_map/all_to_all | solution.py:149
  45.0 53.5 %all-gather = bf16[32,64,20]{1,2,0:T(8,128)(2,1)S(1)} all-gather(bf16[1,64,20]{1,2,0:T(8,128)(2,1)S(1)} %bitcast.496), channel_id=1, replica_groups=mesh['head'=8,'fsdp'=4] {'head','fsdp'}, dimensions={0}, use_global_device_ids=true | all-gather | bytes 84480 | tf_op jit(solution)/shard_map/all_gather | solution.py:142
  127.1 25.3 %collective-permute-done.33 = bf16[128,2048]{1,0:T(8,128)(2,1)} collective-permute-done((bf16[128,2048]{1,0:T(8,128)(2,1)S(1)}, bf16[128,2048]{1,0:T(8,128)(2,1)}, u32[]{:S(2)}, u32[]{:S(2)}) %collective-permute-start.33) | collective-permute-done | bytes 524320 | tf_op jit(solution)/shard_map/ppermute | solution.py:57
  157.2 7.3 collective-permute-done.3
  167.3 8.4 collective-permute-done.35
  179.5 7.4 collective-permute-done.5
  190.6 7.6 collective-permute-done.37
  208.3 5.3 fusion.10
  213.6 7.9 fusion.132
  221.7 20.3 %psum.14 = f32[2,1024]{1,0:T(2,128)} all-reduce(f32[2,1024]{1,0:T(2,128)S(1)} %pad_maximum_fusion.17), channel_id=1, replica_groups=mesh['head'=8,'fsdp'=4] {'head'}, use_global_device_ids=true, to_apply=%region_3.4 | all-reduce | flops 2048 | bytes 16384 | tf_op jit(solution)/shard_map/psum | solution.py:170
  258.6 10.1 %collective-permute-done.8 = bf16[1024,256]{0,1:T(8,128)(2,1)S(1)} collective-permute-done((bf16[1024,256]{0,1:T(8,128)(2,1)S(1)}, bf16[1024,256]{0,1:T(8,128)(2,1)S(1)}, u32[]{:S(2)}, u32[]{:S(2)}) %collective-permute-start.8) | collective-permute-done | bytes 524320 | tf_op jit(solution)/shard_map/ppermute | solution.py:56
  277.1 6.1 collective-permute-done.10
  288.2 6.6 collective-permute-done.12
  302.5 14.3 %multiply_reduce_fusion = (f32[1024]{0:T(1024)S(1)}, f32[1024,2048]{1,0:T(8,128)S(1)}) fusion(bf16[1024,2048]{0,1:T(8,128)(2,1)} %bitcast.38, bf16[2048,2048]{1,0:T(8,128)(2,1)} %all-gather.9.cloned.1.call-done, bf16[8,128,2048]{2,1,0:T(8,128)(2,1)} %fusion.75), kind=kOutput, calls=%fused_computation.30 | convolution fusion | flops 8598322176 | bytes 25169920 | tf_op jit(solution)/shard_map/dot_general | solution.py:103
  323.7 5.6 fusion.4
  329.3 10.0 %fusion.18 = f32[1024,1024]{1,0:T(8,128)} fusion(bf16[1024,2048]{1,0:T(8,128)(2,1)} %copy-done.6, bf16[2,2048,1024]{2,1,0:T(8,128)(2,1)} %all-gather.11.cloned.1.call-done), kind=kOutput, calls=%fused_computation.67 | convolution fusion | flops 4294967296 | bytes 12582912 | tf_op jit(solution)/shard_map/dot_general | solution.py:103
  339.3 6.5 fusion.23
  345.8 10.0 %fusion.20 = f32[1024,1024]{1,0:T(8,128)} fusion(bf16[1024,2048]{1,0:T(8,128)(2,1)} %copy-done.6, bf16[2,2048,1024]{2,1,0:T(8,128)(2,1)} %all-gather.13.cloned.1.call-done), kind=kOutput, calls=%fused_computation.69 | convolution fusion | flops 4294967296 | bytes 12582912 | tf_op jit(solution)/shard_map/dot_general | solution.py:103
  355.9 6.1 fusion.24
  362.0 12.2 %multiply_convert_fusion.5 = (bf16[1024,1024]{1,0:T(8,128)(2,1)S(1)}, bf16[1024,1024]{1,0:T(8,128)(2,1)S(1)}, bf16[1024,1024]{1,0:T(8,128)(2,1)}) fusion(f32[1024,1024]{1,0:T(8,128)} %fusion.18, f32[1024,1024]{1,0:T(8,128)} %fusion.20, bf16[1024,2048]{1,0:T(8,128)(2,1)} %bitcast.454, bf16[2,1024,2048]{2,1,0:T(8,128)(2,1)} %all-gather.15.cloned.1.call-done), kind=kOutput, calls=%fused_computation.49 | convolution fusion | flops 4310695936 | bytes 23068672 | tf_op jit(solution)/shard_map/dot_general | solution.py:103
  374.2 10.4 %fusion.17 = f32[1024,2048]{1,0:T(8,128)} fusion(bf16[1024,1024]{1,0:T(8,128)(2,1)S(1)} %get-tuple-element.89, bf16[2,2048,1024]{2,1,0:T(8,128)(2,1)} %all-gather.11.cloned.1.call-done), kind=kOutput, calls=%fused_computation.66 | convolution fusion | flops 4294967296 | bytes 14680064 | tf_op jit(solution)/shard_map/dot_general | solution.py:103
  384.7 9.1 %fusion.19 = f32[1024,2048]{1,0:T(8,128)} fusion(bf16[1024,1024]{1,0:T(8,128)(2,1)S(1)} %get-tuple-element.88, bf16[2,2048,1024]{2,1,0:T(8,128)(2,1)} %all-gather.13.cloned.1.call-done), kind=kOutput, calls=%fused_computation.68 | convolution fusion | flops 4294967296 | bytes 14680064 | tf_op jit(solution)/shard_map/dot_general | solution.py:103
  393.8 10.4 %multiply_convert_fusion.3 = (bf16[1024,1024]{1,0:T(8,128)(2,1)S(1)}, bf16[1024,1024]{1,0:T(8,128)(2,1)}, bf16[1024,1024]{1,0:T(8,128)(2,1)}) fusion(f32[1024,1024]{1,0:T(8,128)} %fusion.23, f32[1024,1024]{1,0:T(8,128)} %fusion.24, bf16[1024,2048]{1,0:T(8,128)(2,1)S(1)} %bitcast.453, bf16[2,1024,2048]{2,1,0:T(8,128)(2,1)S(1)} %bitcast.530), kind=kOutput, calls=%fused_computation.47 | convolution fusion | flops 4310695936 | bytes 23068672 | tf_op jit(solution)/shard_map/dot_general | solution.py:103
  404.2 9.1 %fusion.22 = f32[1024,2048]{1,0:T(8,128)} fusion(bf16[1024,1024]{1,0:T(8,128)(2,1)} %get-tuple-element.86, bf16[2,2048,1024]{2,1,0:T(8,128)(2,1)S(1)} %bitcast.532), kind=kOutput, calls=%fused_computation.71 | convolution fusion | flops 4294967296 | bytes 14680064 | tf_op jit(solution)/shard_map/dot_general | solution.py:103
  413.4 13.3 %add_convert_fusion = bf16[1024,2048]{1,0:T(8,128)(2,1)} fusion(f32[1024,2048]{1,0:T(8,128)} %fusion.22, f32[1024,2048]{1,0:T(8,128)} %fusion.17, f32[1024,2048]{1,0:T(8,128)} %fusion.19, bf16[1024,1024]{1,0:T(8,128)(2,1)S(1)} %get-tuple-element.85, bf16[2,2048,1024]{2,1,0:T(8,128)(2,1)} %all-gather.13.cloned.1.call-done), kind=kOutput, calls=%fused_computation.28 | convolution fusion | flops 4303355904 | bytes 35651584 | tf_op jit(solution)/shard_map/dot_general | solution.py:103
  430.1 6.9 collective-permute-done.40
  440.5 11.3 %collective-permute-done.41 = bf16[128,2048]{1,0:T(8,128)(2,1)S(1)} collective-permute-done((bf16[128,2048]{1,0:T(8,128)(2,1)S(1)}, bf16[128,2048]{1,0:T(8,128)(2,1)S(1)}, u32[]{:S(2)}, u32[]{:S(2)}) %collective-permute-start.41) | collective-permute-done | bytes 524320 | tf_op jit(solution)/shard_map/ppermute | solution.py:86
  453.3 7.5 convolution_convert_fusion.1
  465.8 12.6 %fusion.2 = (f32[1024]{0:T(1024)S(1)}, f32[1024]{0:T(1024)S(1)}, bf16[1024,2048]{1,0:T(8,128)(2,1)}, bf16[1024,2048]{1,0:T(8,128)(2,1)}, bf16[1024,2048]{1,0:T(8,128)(2,1)}) fusion(bf16[8,128,2048]{2,1,0:T(8,128)(2,1)} %fusion.77, bf16[1024,2048]{1,0:T(8,128)(2,1)S(1)} %convolution_convert_fusion.1, f32[1024]{0:T(1024)S(1)} %bitcast.500, ...), kind=kOutput, calls=%fused_computation.6 | convolution fusion | flops 4328519680 | bytes 27279360 | tf_op jit(solution)/shard_map/dot_general | solution.py:103
  489.6 3.4 collective-permute-done.43
  502.5 6.5 convolution_convert_fusion.4
  509.8 4.6 all-to-all-start.2
  514.9 5.3 fusion.12
  520.1 4.6 all-to-all-done.2
  542.8 19.8 %psum.15 = f32[2,1024]{1,0:T(2,128)S(1)} all-reduce(f32[2,1024]{1,0:T(2,128)S(1)} %pad_maximum_fusion.18), channel_id=1, replica_groups=mesh['head'=8,'fsdp'=4] {'head'}, use_global_device_ids=true, to_apply=%region_23.24 | all-reduce | flops 2048 | bytes 16384 | tf_op jit(solution)/shard_map/psum | solution.py:284
  565.5 4.9 convolution_convert_fusion.3
  570.6 7.6 convert_bitcast_fusion.1
  578.3 6.2 convert_bitcast_fusion
  584.5 6.3 pad_maximum_fusion.2
  590.9 7.6 convert_bitcast_fusion.3
  598.6 6.3 convert_bitcast_fusion.2
  604.9 6.3 pad_maximum_fusion.1
  613.1 7.7 convert_bitcast_fusion.5
  620.8 6.2 convert_bitcast_fusion.4
  627.0 6.2 pad_maximum_fusion
  639.1 4.9 collective-permute-done.24
  647.4 7.6 collective-permute-done.56
  657.2 5.7 convolution_convert_fusion
  663.5 11.3 %collective-permute-done.58 = bf16[128,2048]{1,0:T(8,128)(2,1)S(1)} collective-permute-done((bf16[128,2048]{1,0:T(8,128)(2,1)S(1)}, bf16[128,2048]{1,0:T(8,128)(2,1)S(1)}, u32[]{:S(2)}, u32[]{:S(2)}) %collective-permute-start.58) | collective-permute-done | bytes 524320 | tf_op jit(solution)/shard_map/ppermute | solution.py:56
  677.6 3.5 collective-permute-done.52
  681.4 7.4 collective-permute-done.60
  691.8 8.3 collective-permute-done.49
  700.4 5.4 collective-permute-done.62
  712.0 5.7 collective-permute-done.50
  725.5 3.4 collective-permute-done.54
  747.6 6.8 all-to-all-done.4
  754.4 3.5 all-to-all-start.3
  762.2 23.2 %collective-permute-done.31 = bf16[128,2048]{1,0:T(8,128)(2,1)S(1)} collective-permute-done((bf16[128,2048]{1,0:T(8,128)(2,1)S(1)}, bf16[128,2048]{1,0:T(8,128)(2,1)S(1)}, u32[]{:S(2)}, u32[]{:S(2)}) %collective-permute-start.31) | collective-permute-done | bytes 524320 | tf_op jit(solution)/shard_map/ppermute | solution.py:87
  785.4 4.2 fusion.45
  794.6 4.2 convert_element_type.606
  798.8 4.1 convert_element_type.601
  802.9 26.6 %reduce-scatter.10.cloned.1.call-done = bf16[2,512,1024]{2,1,0:T(8,128)(2,1)} async-done(((bf16[2,2048,1024]{2,1,0:T(8,128)(2,1)}), bf16[2,512,1024]{2,1,0:T(8,128)(2,1)}) %reduce-scatter.10.cloned.1.call-update) | async-done | bytes 2097168 | tf_op jit(solution)/shard_map/reduce_scatter | solution.py:234
  829.5 4.1 convert_element_type.598
  833.5 30.4 %reduce-scatter.8.cloned.1.call-done = f32[64,2048]{1,0:T(8,128)} async-done(((f32[256,2048]{1,0:T(8,128)}), f32[64,2048]{1,0:T(8,128)}) %reduce-scatter.8.cloned.1.call-update) | async-done | bytes 524304 | tf_op jit(solution)/shard_map/reduce_scatter | solution.py:303
  (495 shorter events, 225.7 us)
Async XLA Ops:
  7.2 206.4 %all-gather.7.cloned.1.call-start = ((), (), s32[]{:S(2)}) async-start(), calls=%async_computation.10 | async-start | bytes 3932160 | tf_op jit(solution)/shard_map/all_gather | solution.py:150
  37.5 265.0 %all-gather.9.cloned.1.call-start = ((), (), s32[]{:S(2)}) async-start(), calls=%async_computation.11 | async-start | bytes 8650752 | tf_op jit(solution)/shard_map/all_gather | solution.py:153
  38.2 291.1 %all-gather.11.cloned.1.call-start = ((), (), s32[]{:S(2)}) async-start(), calls=%async_computation.12 | async-start | bytes 10485760 | tf_op jit(solution)/shard_map/all_gather | solution.py:154
  39.0 306.8 %all-gather.13.cloned.1.call-start = ((), (), s32[]{:S(2)}) async-start(), calls=%async_computation.13 | async-start | bytes 10485760 | tf_op jit(solution)/shard_map/all_gather | solution.py:155
  39.5 322.5 %all-gather.15.cloned.1.call-start = ((), (), s32[]{:S(2)}) async-start(), calls=%async_computation.14 | async-start | bytes 10485760 | tf_op jit(solution)/shard_map/all_gather | solution.py:156
  39.6 69.0 %collective-permute-start.16 = (s32[128,16]{0,1:T(8,128)S(1)}, s32[128,16]{0,1:T(8,128)S(1)}, u32[]{:S(2)}, u32[]{:S(2)}) collective-permute-start(s32[128,16]{0,1:T(8,128)S(1)} %pad_add_fusion), channel_id=1, source_target_pairs={{0,8},{8,16},{16,24},{24,28},{28,20},{20,12},{12,4},{4,0},{1,9},{9... | collective-permute-start | bytes 24584 | tf_op jit(solution)/shard_map/ppermute | solution.py:56
  40.8 67.9 %collective-permute-start.17 = (s32[128,16]{0,1:T(8,128)S(1)}, s32[128,16]{0,1:T(8,128)S(1)}, u32[]{:S(2)}, u32[]{:S(2)}) collective-permute-start(s32[128,16]{0,1:T(8,128)S(1)} %pad_add_fusion), channel_id=1, source_target_pairs={{8,0},{16,8},{24,16},{28,24},{20,28},{12,20},{4,12},{0,4},{9,1},{1... | collective-permute-start | bytes 24584 | tf_op jit(solution)/shard_map/ppermute | solution.py:57
  41.7 80.4 %collective-permute-start = (bf16[128,2048]{1,0:T(8,128)(2,1)S(1)}, bf16[128,2048]{1,0:T(8,128)(2,1)S(1)}, u32[]{:S(2)}, u32[]{:S(2)}) collective-permute-start(bf16[128,2048]{1,0:T(8,128)(2,1)S(1)} %bitcast.420), channel_id=1, source_target_pairs={{0,8},{8,16},{16,24},{24,28},{28,20},{20,12},{12,4},{4,0},{1,9},{9... | collective-permute-start | bytes 1572872 | tf_op jit(solution)/shard_map/ppermute | solution.py:56
  42.8 80.6 %collective-permute-start.1 = (bf16[128,2048]{1,0:T(8,128)(2,1)S(1)}, bf16[128,2048]{1,0:T(8,128)(2,1)S(1)}, u32[]{:S(2)}, u32[]{:S(2)}) collective-permute-start(bf16[128,2048]{1,0:T(8,128)(2,1)S(1)} %bitcast.421), channel_id=1, source_target_pairs={{8,0},{16,8},{24,16},{28,24},{20,28},{12,20},{4,12},{0,4},{9,1},{1... | collective-permute-start | bytes 1572872 | tf_op jit(solution)/shard_map/ppermute | solution.py:57
  43.7 82.2 %collective-permute-start.32 = (bf16[128,2048]{1,0:T(8,128)(2,1)S(1)}, bf16[128,2048]{1,0:T(8,128)(2,1)S(1)}, u32[]{:S(2)}, u32[]{:S(2)}) collective-permute-start(bf16[128,2048]{1,0:T(8,128)(2,1)S(1)} %bitcast.434), channel_id=1, source_target_pairs={{0,8},{8,16},{16,24},{24,28},{28,20},{20,12},{12,4},{4,0},{1,9},{9... | collective-permute-start | bytes 1572872 | tf_op jit(solution)/shard_map/ppermute | solution.py:56
  120.3 32.1 %collective-permute-start.33 = (bf16[128,2048]{1,0:T(8,128)(2,1)S(1)}, bf16[128,2048]{1,0:T(8,128)(2,1)}, u32[]{:S(2)}, u32[]{:S(2)}) collective-permute-start(bf16[128,2048]{1,0:T(8,128)(2,1)S(1)} %bitcast.435), channel_id=1, source_target_pairs={{8,0},{16,8},{24,16},{28,24},{20,28},{12,20},{4,12},{0,4},{9,1},{1... | collective-permute-start | bytes 1572872 | tf_op jit(solution)/shard_map/ppermute | solution.py:57
  122.2 32.2 %collective-permute-start.2 = (bf16[128,2048]{1,0:T(8,128)(2,1)S(1)}, bf16[128,2048]{1,0:T(8,128)(2,1)S(1)}, u32[]{:S(2)}, u32[]{:S(2)}) collective-permute-start(bf16[128,2048]{1,0:T(8,128)(2,1)S(1)} %collective-permute-done), channel_id=1, source_target_pairs={{0,8},{8,16},{16,24},{24,28},{28,20},{20,12},{12,4},{4,0},{1,9},{9... | collective-permute-start | bytes 1572872 | tf_op jit(solution)/shard_map/ppermute | solution.py:56
  123.4 41.0 %collective-permute-start.3 = (bf16[128,2048]{1,0:T(8,128)(2,1)S(1)}, bf16[128,2048]{1,0:T(8,128)(2,1)S(1)}, u32[]{:S(2)}, u32[]{:S(2)}) collective-permute-start(bf16[128,2048]{1,0:T(8,128)(2,1)S(1)} %collective-permute-done.1), channel_id=1, source_target_pairs={{8,0},{16,8},{24,16},{28,24},{20,28},{12,20},{4,12},{0,4},{9,1},{1... | collective-permute-start | bytes 1572872 | tf_op jit(solution)/shard_map/ppermute | solution.py:57
  125.9 38.7 %collective-permute-start.34 = (bf16[128,2048]{1,0:T(8,128)(2,1)S(1)}, bf16[128,2048]{1,0:T(8,128)(2,1)S(1)}, u32[]{:S(2)}, u32[]{:S(2)}) collective-permute-start(bf16[128,2048]{1,0:T(8,128)(2,1)S(1)} %collective-permute-done.32), channel_id=1, source_target_pairs={{0,8},{8,16},{16,24},{24,28},{28,20},{20,12},{12,4},{4,0},{1,9},{9... | collective-permute-start | bytes 1572872 | tf_op jit(solution)/shard_map/ppermute | solution.py:56
  152.4 23.3 %collective-permute-start.35 = (bf16[128,2048]{1,0:T(8,128)(2,1)}, bf16[128,2048]{1,0:T(8,128)(2,1)S(1)}, u32[]{:S(2)}, u32[]{:S(2)}) collective-permute-start(bf16[128,2048]{1,0:T(8,128)(2,1)} %collective-permute-done.33), channel_id=1, source_target_pairs={{8,0},{16,8},{24,16},{28,24},{20,28},{12,20},{4,12},{0,4},{9,1},{1... | collective-permute-start | bytes 1572872 | tf_op jit(solution)/shard_map/ppermute | solution.py:57
  154.3 23.2 %collective-permute-start.4 = (bf16[128,2048]{1,0:T(8,128)(2,1)S(1)}, bf16[128,2048]{1,0:T(8,128)(2,1)S(1)}, u32[]{:S(2)}, u32[]{:S(2)}) collective-permute-start(bf16[128,2048]{1,0:T(8,128)(2,1)S(1)} %collective-permute-done.2), channel_id=1, source_target_pairs={{0,8},{8,16},{16,24},{24,28},{28,20},{20,12},{12,4},{4,0},{1,9},{9... | collective-permute-start | bytes 1572872 | tf_op jit(solution)/shard_map/ppermute | solution.py:56
  164.5 22.5 %collective-permute-start.5 = (bf16[128,2048]{1,0:T(8,128)(2,1)S(1)}, bf16[128,2048]{1,0:T(8,128)(2,1)S(1)}, u32[]{:S(2)}, u32[]{:S(2)}) collective-permute-start(bf16[128,2048]{1,0:T(8,128)(2,1)S(1)} %collective-permute-done.3), channel_id=1, source_target_pairs={{8,0},{16,8},{24,16},{28,24},{20,28},{12,20},{4,12},{0,4},{9,1},{1... | collective-permute-start | bytes 1572872 | tf_op jit(solution)/shard_map/ppermute | solution.py:57
  164.6 22.5 %collective-permute-start.36 = (bf16[128,2048]{1,0:T(8,128)(2,1)S(1)}, bf16[128,2048]{1,0:T(8,128)(2,1)S(1)}, u32[]{:S(2)}, u32[]{:S(2)}) collective-permute-start(bf16[128,2048]{1,0:T(8,128)(2,1)S(1)} %collective-permute-done.34), channel_id=1, source_target_pairs={{0,8},{8,16},{16,24},{24,28},{28,20},{20,12},{12,4},{4,0},{1,9},{9... | collective-permute-start | bytes 1572872 | tf_op jit(solution)/shard_map/ppermute | solution.py:56
  175.7 22.5 %collective-permute-start.37 = (bf16[128,2048]{1,0:T(8,128)(2,1)S(1)}, bf16[128,2048]{1,0:T(8,128)(2,1)S(1)}, u32[]{:S(2)}, u32[]{:S(2)}) collective-permute-start(bf16[128,2048]{1,0:T(8,128)(2,1)S(1)} %collective-permute-done.35), channel_id=1, source_target_pairs={{8,0},{16,8},{24,16},{28,24},{20,28},{12,20},{4,12},{0,4},{9,1},{1... | collective-permute-start | bytes 1572872 | tf_op jit(solution)/shard_map/ppermute | solution.py:57
  177.6 24.3 %collective-permute-start.6 = (bf16[64,2048]{1,0:T(8,128)(2,1)S(1)}, bf16[64,2048]{1,0:T(8,128)(2,1)S(1)}, u32[]{:S(2)}, u32[]{:S(2)}) collective-permute-start(bf16[64,2048]{1,0:T(8,128)(2,1)S(1)} %slice.410), channel_id=1, source_target_pairs={{0,8},{8,16},{16,24},{24,28},{28,20},{20,12},{12,4},{4,0},{1,9},{9... | collective-permute-start | bytes 786440 | tf_op jit(solution)/shard_map/ppermute | solution.py:60
  187.0 16.8 %collective-permute-start.7 = (bf16[64,2048]{1,0:T(8,128)(2,1)S(1)}, bf16[64,2048]{1,0:T(8,128)(2,1)S(1)}, u32[]{:S(2)}, u32[]{:S(2)}) collective-permute-start(bf16[64,2048]{1,0:T(8,128)(2,1)S(1)} %slice.411), channel_id=1, source_target_pairs={{8,0},{16,8},{24,16},{28,24},{20,28},{12,20},{4,12},{0,4},{9,1},{1... | collective-permute-start | bytes 786440 | tf_op jit(solution)/shard_map/ppermute | solution.py:61
  188.6 82.4 %collective-permute-start.38 = (bf16[64,2048]{1,0:T(8,128)(2,1)}, bf16[64,2048]{1,0:T(8,128)(2,1)}, u32[]{:S(2)}, u32[]{:S(2)}) collective-permute-start(bf16[64,2048]{1,0:T(8,128)(2,1)} %slice.443), channel_id=1, source_target_pairs={{0,8},{8,16},{16,24},{24,28},{28,20},{20,12},{12,4},{4,0},{1,9},{9... | collective-permute-start | bytes 786440 | tf_op jit(solution)/shard_map/ppermute | solution.py:60
  199.7 71.3 %collective-permute-start.39 = (bf16[64,2048]{1,0:T(8,128)(2,1)}, bf16[64,2048]{1,0:T(8,128)(2,1)}, u32[]{:S(2)}, u32[]{:S(2)}) collective-permute-start(bf16[64,2048]{1,0:T(8,128)(2,1)} %slice.444), channel_id=1, source_target_pairs={{8,0},{16,8},{24,16},{28,24},{20,28},{12,20},{4,12},{0,4},{9,1},{1... | collective-permute-start | bytes 786440 | tf_op jit(solution)/shard_map/ppermute | solution.py:61
  254.6 14.0 %collective-permute-start.8 = (bf16[1024,256]{0,1:T(8,128)(2,1)S(1)}, bf16[1024,256]{0,1:T(8,128)(2,1)S(1)}, u32[]{:S(2)}, u32[]{:S(2)}) collective-permute-start(bf16[1024,256]{0,1:T(8,128)(2,1)S(1)} %pad_maximum_fusion.8), channel_id=1, source_target_pairs={{0,8},{8,16},{16,24},{24,28},{28,20},{20,12},{12,4},{4,0},{1,9},{9... | collective-permute-start | bytes 1572872 | tf_op jit(solution)/shard_map/ppermute | solution.py:56
  254.9 13.9 %collective-permute-start.9 = (bf16[1024,256]{0,1:T(8,128)(2,1)S(1)}, bf16[1024,256]{0,1:T(8,128)(2,1)S(1)}, u32[]{:S(2)}, u32[]{:S(2)}) collective-permute-start(bf16[1024,256]{0,1:T(8,128)(2,1)S(1)} %pad_maximum_fusion.8), channel_id=1, source_target_pairs={{8,0},{16,8},{24,16},{28,24},{20,28},{12,20},{4,12},{0,4},{9,1},{1... | collective-permute-start | bytes 1572872 | tf_op jit(solution)/shard_map/ppermute | solution.py:57
  268.7 14.6 %collective-permute-start.10 = (bf16[1024,256]{0,1:T(8,128)(2,1)S(1)}, bf16[1024,256]{0,1:T(8,128)(2,1)S(1)}, u32[]{:S(2)}, u32[]{:S(2)}) collective-permute-start(bf16[1024,256]{0,1:T(8,128)(2,1)S(1)} %collective-permute-done.8), channel_id=1, source_target_pairs={{0,8},{8,16},{16,24},{24,28},{28,20},{20,12},{12,4},{4,0},{1,9},{9... | collective-permute-start | bytes 1572872 | tf_op jit(solution)/shard_map/ppermute | solution.py:56
  268.8 14.6 %collective-permute-start.11 = (bf16[1024,256]{0,1:T(8,128)(2,1)S(1)}, bf16[1024,256]{0,1:T(8,128)(2,1)S(1)}, u32[]{:S(2)}, u32[]{:S(2)}) collective-permute-start(bf16[1024,256]{0,1:T(8,128)(2,1)S(1)} %collective-permute-done.9), channel_id=1, source_target_pairs={{8,0},{16,8},{24,16},{28,24},{20,28},{12,20},{4,12},{0,4},{9,1},{1... | collective-permute-start | bytes 1572872 | tf_op jit(solution)/shard_map/ppermute | solution.py:57
  283.2 11.6 %collective-permute-start.12 = (bf16[1024,256]{0,1:T(8,128)(2,1)S(1)}, bf16[1024,256]{0,1:T(8,128)(2,1)S(1)}, u32[]{:S(2)}, u32[]{:S(2)}) collective-permute-start(bf16[1024,256]{0,1:T(8,128)(2,1)S(1)} %collective-permute-done.10), channel_id=1, source_target_pairs={{0,8},{8,16},{16,24},{24,28},{28,20},{20,12},{12,4},{4,0},{1,9},{9... | collective-permute-start | bytes 1572872 | tf_op jit(solution)/shard_map/ppermute | solution.py:56
  283.3 11.8 %collective-permute-start.13 = (bf16[1024,256]{0,1:T(8,128)(2,1)S(1)}, bf16[1024,256]{0,1:T(8,128)(2,1)S(1)}, u32[]{:S(2)}, u32[]{:S(2)}) collective-permute-start(bf16[1024,256]{0,1:T(8,128)(2,1)S(1)} %collective-permute-done.11), channel_id=1, source_target_pairs={{8,0},{16,8},{24,16},{28,24},{20,28},{12,20},{4,12},{0,4},{9,1},{1... | collective-permute-start | bytes 1572872 | tf_op jit(solution)/shard_map/ppermute | solution.py:57
  438.3 13.5 %collective-permute-start.41 = (bf16[128,2048]{1,0:T(8,128)(2,1)S(1)}, bf16[128,2048]{1,0:T(8,128)(2,1)S(1)}, u32[]{:S(2)}, u32[]{:S(2)}) collective-permute-start(bf16[128,2048]{1,0:T(8,128)(2,1)S(1)} %pad_maximum_fusion.11), channel_id=1, source_target_pairs={{0,8},{8,16},{16,24},{24,28},{28,20},{20,12},{12,4},{4,0},{1,9},{9... | collective-permute-start | bytes 1572872 | tf_op jit(solution)/shard_map/ppermute | solution.py:86
  438.6 22.2 %collective-permute-start.45 = (bf16[128,2048]{1,0:T(8,128)(2,1)S(1)}, bf16[128,2048]{1,0:T(8,128)(2,1)S(1)}, u32[]{:S(2)}, u32[]{:S(2)}) collective-permute-start(bf16[128,2048]{1,0:T(8,128)(2,1)S(1)} %pad_maximum_fusion.12), channel_id=1, source_target_pairs={{8,0},{16,8},{24,16},{28,24},{20,28},{12,20},{4,12},{0,4},{9,1},{1... | collective-permute-start | bytes 1572872 | tf_op jit(solution)/shard_map/ppermute | solution.py:87
  453.0 9.2 %collective-permute-start.42 = (bf16[128,2048]{1,0:T(8,128)(2,1)S(1)}, bf16[128,2048]{1,0:T(8,128)(2,1)S(1)}, u32[]{:S(2)}, u32[]{:S(2)}) collective-permute-start(bf16[128,2048]{1,0:T(8,128)(2,1)S(1)} %fusion.55), channel_id=1, source_target_pairs={{0,8},{8,16},{16,24},{24,28},{28,20},{20,12},{12,4},{4,0},{1,9},{9... | collective-permute-start | bytes 1572872 | tf_op jit(solution)/shard_map/ppermute | solution.py:86
  463.8 21.9 %collective-permute-start.46 = (bf16[128,2048]{1,0:T(8,128)(2,1)S(1)}, bf16[128,2048]{1,0:T(8,128)(2,1)S(1)}, u32[]{:S(2)}, u32[]{:S(2)}) collective-permute-start(bf16[128,2048]{1,0:T(8,128)(2,1)S(1)} %get-tuple-element.103), channel_id=1, source_target_pairs={{8,0},{16,8},{24,16},{28,24},{20,28},{12,20},{4,12},{0,4},{9,1},{1... | collective-permute-start | bytes 1572872 | tf_op jit(solution)/shard_map/ppermute | solution.py:87
  479.0 9.9 %all-to-all-start.1 = ((f32[8,2,128]{2,1,0:T(2,128)}), f32[8,2,128]{2,1,0:T(2,128)S(1)}, u32[]{:S(2)}, u32[]{:S(2)}) async-start(f32[8,2,128]{2,1,0:T(2,128)} %maximum_bitcast_fusion.4), calls=%async_computation.1 | async-start | bytes 16384 | tf_op jit(solution)/shard_map/all_to_all | solution.py:242
  483.7 9.2 %collective-permute-start.43 = (bf16[128,2048]{1,0:T(8,128)(2,1)S(1)}, bf16[128,2048]{1,0:T(8,128)(2,1)S(1)}, u32[]{:S(2)}, u32[]{:S(2)}) collective-permute-start(bf16[128,2048]{1,0:T(8,128)(2,1)S(1)} %get-tuple-element.102), channel_id=1, source_target_pairs={{0,8},{8,16},{16,24},{24,28},{28,20},{20,12},{12,4},{4,0},{1,9},{9... | collective-permute-start | bytes 1572872 | tf_op jit(solution)/shard_map/ppermute | solution.py:86
  486.9 9.2 %collective-permute-start.47 = (bf16[128,2048]{1,0:T(8,128)(2,1)S(1)}, bf16[128,2048]{1,0:T(8,128)(2,1)S(1)}, u32[]{:S(2)}, u32[]{:S(2)}) collective-permute-start(bf16[128,2048]{1,0:T(8,128)(2,1)S(1)} %fusion.54), channel_id=1, source_target_pairs={{8,0},{16,8},{24,16},{28,24},{20,28},{12,20},{4,12},{0,4},{9,1},{1... | collective-permute-start | bytes 1572872 | tf_op jit(solution)/shard_map/ppermute | solution.py:87
  509.8 14.9 %all-to-all-start.2 = ((bf16[128,8,256]{2,0,1:T(8,128)(2,1)}), bf16[128,8,256]{2,0,1:T(8,128)(2,1)S(1)}, u32[]{:S(2)}, u32[]{:S(2)}) async-start(bf16[128,8,256]{2,0,1:T(8,128)(2,1)} %bitcast.414), calls=%async_computation.2 | async-start | bytes 1048576 | tf_op jit(solution)/shard_map/all_to_all | solution.py:264
  514.4 240.0 %reduce-scatter.6.cloned.1.call-start = ((), (), s32[]{:S(2)}) async-start(), calls=%async_computation.15 | async-start | bytes 3932160 | tf_op jit(solution)/shard_map/reduce_scatter | solution.py:298
  570.4 224.3 %reduce-scatter.14.cloned.1.call-start = ((), (), s32[]{:S(2)}) async-start(), calls=%async_computation.19 | async-start | bytes 10485760 | tf_op jit(solution)/shard_map/reduce_scatter | solution.py:234
  590.8 208.0 %reduce-scatter.12.cloned.1.call-start = ((), (), s32[]{:S(2)}) async-start(), calls=%async_computation.18 | async-start | bytes 10485760 | tf_op jit(solution)/shard_map/reduce_scatter | solution.py:234
  611.2 218.3 %reduce-scatter.10.cloned.1.call-start = ((), (), s32[]{:S(2)}) async-start(), calls=%async_computation.17 | async-start | bytes 10485760 | tf_op jit(solution)/shard_map/reduce_scatter | solution.py:234
  633.2 230.7 %reduce-scatter.8.cloned.1.call-start = ((), (), s32[]{:S(2)}) async-start(), calls=%async_computation.16 | async-start | bytes 2621440 | tf_op jit(solution)/shard_map/reduce_scatter | solution.py:303
  634.7 9.3 %collective-permute-start.24 = (bf16[64,2048]{1,0:T(8,128)(2,1)S(1)}, bf16[64,2048]{1,0:T(8,128)(2,1)S(1)}, u32[]{:S(2)}, u32[]{:S(2)}) collective-permute-start(bf16[64,2048]{1,0:T(8,128)(2,1)S(1)} %get-tuple-element.116), channel_id=1, source_target_pairs={{0,8},{8,16},{16,24},{24,28},{28,20},{20,12},{12,4},{4,0},{1,9},{9... | collective-permute-start | bytes 786440 | tf_op jit(solution)/shard_map/ppermute | solution.py:75
  637.0 18.0 %collective-permute-start.56 = (bf16[128,2048]{1,0:T(8,128)(2,1)S(1)}, bf16[128,2048]{1,0:T(8,128)(2,1)S(1)}, u32[]{:S(2)}, u32[]{:S(2)}) collective-permute-start(bf16[128,2048]{1,0:T(8,128)(2,1)S(1)} %copy-done.37), channel_id=1, source_target_pairs={{0,8},{8,16},{16,24},{24,28},{28,20},{20,12},{12,4},{4,0},{1,9},{9... | collective-permute-start | bytes 1572872 | tf_op jit(solution)/shard_map/ppermute | solution.py:56
  637.1 18.1 %collective-permute-start.57 = (bf16[128,2048]{1,0:T(8,128)(2,1)S(1)}, bf16[128,2048]{1,0:T(8,128)(2,1)S(1)}, u32[]{:S(2)}, u32[]{:S(2)}) collective-permute-start(bf16[128,2048]{1,0:T(8,128)(2,1)S(1)} %copy-done.37), channel_id=1, source_target_pairs={{8,0},{16,8},{24,16},{28,24},{20,28},{12,20},{4,12},{0,4},{9,1},{1... | collective-permute-start | bytes 1572872 | tf_op jit(solution)/shard_map/ppermute | solution.py:57
  645.2 85.1 %collective-permute-start.29 = (bf16[128,2048]{1,0:T(8,128)(2,1)S(1)}, bf16[128,2048]{1,0:T(8,128)(2,1)}, u32[]{:S(2)}, u32[]{:S(2)}) collective-permute-start(bf16[128,2048]{1,0:T(8,128)(2,1)S(1)} %pad_maximum_fusion.10), channel_id=1, source_target_pairs={{8,0},{16,8},{24,16},{28,24},{20,28},{12,20},{4,12},{0,4},{9,1},{1... | collective-permute-start | bytes 1572872 | tf_op jit(solution)/shard_map/ppermute | solution.py:87
  645.4 74.5 %collective-permute-start.25 = (bf16[128,2048]{1,0:T(8,128)(2,1)S(1)}, bf16[128,2048]{1,0:T(8,128)(2,1)S(1)}, u32[]{:S(2)}, u32[]{:S(2)}) collective-permute-start(bf16[128,2048]{1,0:T(8,128)(2,1)S(1)} %pad_maximum_fusion.9), channel_id=1, source_target_pairs={{0,8},{8,16},{16,24},{24,28},{28,20},{20,12},{12,4},{4,0},{1,9},{9... | collective-permute-start | bytes 1572872 | tf_op jit(solution)/shard_map/ppermute | solution.py:86
  655.1 19.7 %collective-permute-start.58 = (bf16[128,2048]{1,0:T(8,128)(2,1)S(1)}, bf16[128,2048]{1,0:T(8,128)(2,1)S(1)}, u32[]{:S(2)}, u32[]{:S(2)}) collective-permute-start(bf16[128,2048]{1,0:T(8,128)(2,1)S(1)} %collective-permute-done.56), channel_id=1, source_target_pairs={{0,8},{8,16},{16,24},{24,28},{28,20},{20,12},{12,4},{4,0},{1,9},{9... | collective-permute-start | bytes 1572872 | tf_op jit(solution)/shard_map/ppermute | solution.py:56
  655.3 19.5 %collective-permute-start.59 = (bf16[128,2048]{1,0:T(8,128)(2,1)S(1)}, bf16[128,2048]{1,0:T(8,128)(2,1)S(1)}, u32[]{:S(2)}, u32[]{:S(2)}) collective-permute-start(bf16[128,2048]{1,0:T(8,128)(2,1)S(1)} %collective-permute-done.57), channel_id=1, source_target_pairs={{8,0},{16,8},{24,16},{28,24},{20,28},{12,20},{4,12},{0,4},{9,1},{1... | collective-permute-start | bytes 1572872 | tf_op jit(solution)/shard_map/ppermute | solution.py:57
  663.0 14.6 %collective-permute-start.48 = (bf16[64,2048]{1,0:T(8,128)(2,1)S(1)}, bf16[64,2048]{1,0:T(8,128)(2,1)S(1)}, u32[]{:S(2)}, u32[]{:S(2)}) collective-permute-start(bf16[64,2048]{1,0:T(8,128)(2,1)S(1)} %get-tuple-element.98), channel_id=1, source_target_pairs={{0,8},{8,16},{16,24},{24,28},{28,20},{20,12},{12,4},{4,0},{1,9},{9... | collective-permute-start | bytes 786440 | tf_op jit(solution)/shard_map/ppermute | solution.py:75
  674.8 14.0 %collective-permute-start.60 = (bf16[128,2048]{1,0:T(8,128)(2,1)S(1)}, bf16[128,2048]{1,0:T(8,128)(2,1)S(1)}, u32[]{:S(2)}, u32[]{:S(2)}) collective-permute-start(bf16[128,2048]{1,0:T(8,128)(2,1)S(1)} %collective-permute-done.58), channel_id=1, source_target_pairs={{0,8},{8,16},{16,24},{24,28},{28,20},{20,12},{12,4},{4,0},{1,9},{9... | collective-permute-start | bytes 1572872 | tf_op jit(solution)/shard_map/ppermute | solution.py:56
  677.6 11.8 %collective-permute-start.61 = (bf16[128,2048]{1,0:T(8,128)(2,1)S(1)}, bf16[128,2048]{1,0:T(8,128)(2,1)S(1)}, u32[]{:S(2)}, u32[]{:S(2)}) collective-permute-start(bf16[128,2048]{1,0:T(8,128)(2,1)S(1)} %collective-permute-done.59), channel_id=1, source_target_pairs={{8,0},{16,8},{24,16},{28,24},{20,28},{12,20},{4,12},{0,4},{9,1},{1... | collective-permute-start | bytes 1572872 | tf_op jit(solution)/shard_map/ppermute | solution.py:57
  681.3 30.7 %collective-permute-start.53 = (bf16[128,2048]{1,0:T(8,128)(2,1)S(1)}, bf16[128,2048]{1,0:T(8,128)(2,1)}, u32[]{:S(2)}, u32[]{:S(2)}) collective-permute-start(bf16[128,2048]{1,0:T(8,128)(2,1)S(1)} %pad_maximum_fusion.14), channel_id=1, source_target_pairs={{8,0},{16,8},{24,16},{28,24},{20,28},{12,20},{4,12},{0,4},{9,1},{1... | collective-permute-start | bytes 1572872 | tf_op jit(solution)/shard_map/ppermute | solution.py:87
  688.8 11.4 %collective-permute-start.49 = (bf16[128,2048]{1,0:T(8,128)(2,1)S(1)}, bf16[128,2048]{1,0:T(8,128)(2,1)S(1)}, u32[]{:S(2)}, u32[]{:S(2)}) collective-permute-start(bf16[128,2048]{1,0:T(8,128)(2,1)S(1)} %pad_maximum_fusion.13), channel_id=1, source_target_pairs={{0,8},{8,16},{16,24},{24,28},{28,20},{20,12},{12,4},{4,0},{1,9},{9... | collective-permute-start | bytes 1572872 | tf_op jit(solution)/shard_map/ppermute | solution.py:86
  689.4 16.4 %collective-permute-start.62 = (bf16[64,2048]{1,0:T(8,128)(2,1)S(1)}, bf16[64,2048]{1,0:T(8,128)(2,1)S(1)}, u32[]{:S(2)}, u32[]{:S(2)}) collective-permute-start(bf16[64,2048]{1,0:T(8,128)(2,1)S(1)} %slice.453), channel_id=1, source_target_pairs={{0,8},{8,16},{16,24},{24,28},{28,20},{20,12},{12,4},{4,0},{1,9},{9... | collective-permute-start | bytes 786440 | tf_op jit(solution)/shard_map/ppermute | solution.py:60
  705.8 12.0 %collective-permute-start.50 = (bf16[128,2048]{1,0:T(8,128)(2,1)S(1)}, bf16[128,2048]{1,0:T(8,128)(2,1)}, u32[]{:S(2)}, u32[]{:S(2)}) collective-permute-start(bf16[128,2048]{1,0:T(8,128)(2,1)S(1)} %fusion.50), channel_id=1, source_target_pairs={{0,8},{8,16},{16,24},{24,28},{28,20},{20,12},{12,4},{4,0},{1,9},{9... | collective-permute-start | bytes 1572872 | tf_op jit(solution)/shard_map/ppermute | solution.py:86
  719.6 9.2 %collective-permute-start.54 = (bf16[128,2048]{1,0:T(8,128)(2,1)S(1)}, bf16[128,2048]{1,0:T(8,128)(2,1)S(1)}, u32[]{:S(2)}, u32[]{:S(2)}) collective-permute-start(bf16[128,2048]{1,0:T(8,128)(2,1)S(1)} %get-tuple-element.95), channel_id=1, source_target_pairs={{8,0},{16,8},{24,16},{28,24},{20,28},{12,20},{4,12},{0,4},{9,1},{1... | collective-permute-start | bytes 1572872 | tf_op jit(solution)/shard_map/ppermute | solution.py:87
  721.1 9.5 %collective-permute-start.26 = (bf16[128,2048]{1,0:T(8,128)(2,1)S(1)}, bf16[128,2048]{1,0:T(8,128)(2,1)S(1)}, u32[]{:S(2)}, u32[]{:S(2)}) collective-permute-start(bf16[128,2048]{1,0:T(8,128)(2,1)S(1)} %fusion.61), channel_id=1, source_target_pairs={{0,8},{8,16},{16,24},{24,28},{28,20},{20,12},{12,4},{4,0},{1,9},{9... | collective-permute-start | bytes 1572872 | tf_op jit(solution)/shard_map/ppermute | solution.py:86
  724.6 11.6 %collective-permute-start.51 = (bf16[128,2048]{1,0:T(8,128)(2,1)S(1)}, bf16[128,2048]{1,0:T(8,128)(2,1)S(1)}, u32[]{:S(2)}, u32[]{:S(2)}) collective-permute-start(bf16[128,2048]{1,0:T(8,128)(2,1)S(1)} %get-tuple-element.94), channel_id=1, source_target_pairs={{0,8},{8,16},{16,24},{24,28},{28,20},{20,12},{12,4},{4,0},{1,9},{9... | collective-permute-start | bytes 1572872 | tf_op jit(solution)/shard_map/ppermute | solution.py:86
  733.4 24.5 %collective-permute-start.30 = (bf16[128,2048]{1,0:T(8,128)(2,1)}, bf16[128,2048]{1,0:T(8,128)(2,1)}, u32[]{:S(2)}, u32[]{:S(2)}) collective-permute-start(bf16[128,2048]{1,0:T(8,128)(2,1)} %get-tuple-element.113), channel_id=1, source_target_pairs={{8,0},{16,8},{24,16},{28,24},{20,28},{12,20},{4,12},{0,4},{9,1},{1... | collective-permute-start | bytes 1572872 | tf_op jit(solution)/shard_map/ppermute | solution.py:87
  743.1 11.2 %all-to-all-start.4 = ((f32[32,1,1280]{2,1,0:T(1,128)}), f32[32,1,1280]{2,1,0:T(1,128)S(1)}, u32[]{:S(2)}, u32[]{:S(2)}) async-start(f32[32,1,1280]{2,1,0:T(1,128)} %all_to_all.34), calls=%async_computation.6 | async-start | bytes 327680 | tf_op jit(solution)/shard_map/all_to_all | solution.py:320
  745.8 16.4 %collective-permute-start.27 = (bf16[128,2048]{1,0:T(8,128)(2,1)}, bf16[128,2048]{1,0:T(8,128)(2,1)}, u32[]{:S(2)}, u32[]{:S(2)}) collective-permute-start(bf16[128,2048]{1,0:T(8,128)(2,1)} %get-tuple-element.112), channel_id=1, source_target_pairs={{0,8},{8,16},{16,24},{24,28},{28,20},{20,12},{12,4},{4,0},{1,9},{9... | collective-permute-start | bytes 1572872 | tf_op jit(solution)/shard_map/ppermute | solution.py:86
  754.4 36.8 %all-to-all-start.3 = ((bf16[8,64,768]{2,1,0:T(8,128)(2,1)}), bf16[8,64,768]{2,1,0:T(8,128)(2,1)S(1)}, u32[]{:S(2)}, u32[]{:S(2)}) async-start(bf16[8,64,768]{2,1,0:T(8,128)(2,1)} %reduce-scatter.6.cloned.1.call-done), calls=%async_computation.4 | async-start | bytes 1572864 | tf_op jit(solution)/shard_map/all_to_all | solution.py:299
  759.3 26.1 %collective-permute-start.31 = (bf16[128,2048]{1,0:T(8,128)(2,1)S(1)}, bf16[128,2048]{1,0:T(8,128)(2,1)S(1)}, u32[]{:S(2)}, u32[]{:S(2)}) collective-permute-start(bf16[128,2048]{1,0:T(8,128)(2,1)S(1)} %fusion.60), channel_id=1, source_target_pairs={{8,0},{16,8},{24,16},{28,24},{20,28},{12,20},{4,12},{0,4},{9,1},{1... | collective-permute-start | bytes 1572872 | tf_op jit(solution)/shard_map/ppermute | solution.py:87
  (109 other events, 1578.0 us)
Sparse Core Ops, SparseCore 0:
  37.6 28.0 all-gather.6
  68.6 92.0 all-gather.8
  162.2 65.0 all-gather.10
  228.8 58.2 all-gather.12
  288.5 58.2 all-gather.14
  570.5 33.8 reduce-scatter.5
  607.1 71.6 reduce-scatter.13
  681.4 73.4 reduce-scatter.11
  757.6 71.7 reduce-scatter.9
  832.4 31.4 reduce-scatter.7
where the time goes:
time: 878 us; the launch traced here: 871 us
  waiting for transfers between devices  278 us (32%)
  matrix products  220 us (25%)
  blocking collectives  121 us (14%)
  other arithmetic  99 us (11%)
  starting transfers between devices  79 us (9%)
  local copies, waits for them, and re-layouts  56.9 us (6%)
  between operations  17.3 us (2%)
    dot_general x37, matrix products, dot(): return lax.dot_general(a, b, (dims, ((), ())), preferred_element_type=F32)  218 us
    ppermute x15, waiting for transfers between devices, gather_ring(): l = lax.ppermute(l, 'head', left)  58.9 us
    all_gather x1, blocking collectives, body(): small = lax.all_gather(small, both, axis=0, tiled=True)  53.5 us
    ppermute x15, waiting for transfers between devices, gather_ring(): r = lax.ppermute(r, 'head', right)  49.1 us
    ppermute x9, waiting for transfers between devices, scatter_ring(): r = lax.ppermute(br.astype(BF), 'head', right)  34.1 us
    ppermute x9, waiting for transfers between devices, scatter_ring(): l = lax.ppermute(bl.astype(BF), 'head', left)  32.8 us
    reduce_scatter x1, waiting for transfers between devices, body(): lax.psum_scatter(grad_out_w, 'fsdp', scatter_dimension=0, tiled=True)  30.4 us
    all_to_all x1, blocking collectives, body(): cols = lax.all_to_all(cols, 'head', split_axis=0, concat_axis=0, tiled=True)  27.5 us
  transfers between devices with their start and end apart: 78, of which 43 were waited for; matrix products, arithmetic and copies ran while one was open for 29% of the time, Pallas kernels for 0%

commit v1 on v0

--- a/solution.py
+++ b/solution.py
@@ -167,7 +167,8 @@
     proj_q = projected[:, :dh]
     proj_k = projected[:, dh : 2 * dh]
     squares = jnp.stack([jnp.sum(proj_q * proj_q, axis=1), jnp.sum(proj_k * proj_k, axis=1)])
-    squares = lax.psum(squares, "head") / width
+    resolve_routes_all = lambda frame_in: jnp.sum(jax.lax.all_gather(frame_in, "head"), 0)
+    squares = resolve_routes_all(squares) / width
     inv_q = lax.rsqrt(squares[0] + EPS)[:, None]
     inv_k = lax.rsqrt(squares[1] + EPS)[:, None]
     frequency = ROPE_BASE ** (-2.0 * jnp.arange(HD // 2, dtype=F32) / HD)

time: 878 us -> 887 us (1.010)
  blocking collectives: 121 us -> 134 us
    all_gather x0 -> x1, blocking collectives: none -> 33 us  [body(): jax.lax.all_gather(frame_in, 'head')]
    psum x1 -> x0, blocking collectives: 20.3 us -> none  [body(): squares = lax.psum(squares, 'head') / width]
  transfers between devices with their start and end apart: 78 -> 78, of which waited for: 43 -> 44; matrix products, arithmetic and copies ran while one was open for 29% -> 29% of each run, Pallas kernels for 0% -> 0%
where the time goes in v1:
time: 887 us; the launch traced here: 880 us
  waiting for transfers between devices  279 us (31%)
  matrix products  220 us (25%)
  blocking collectives  134 us (15%)
  other arithmetic  99 us (11%)
  starting transfers between devices  74.9 us (8%)
  local copies, waits for them, and re-layouts  56.9 us (6%)
  between operations  17.1 us (2%)
    dot_general x37, matrix products, dot(): return lax.dot_general(a, b, (dims, ((), ())), preferred_element_type=F32)  218 us
    ppermute x15, waiting for transfers between devices, gather_ring(): l = lax.ppermute(l, 'head', left)  62 us
    all_gather x1, blocking collectives, body(): small = lax.all_gather(small, both, axis=0, tiled=True)  53.5 us
    ppermute x15, waiting for transfers between devices, gather_ring(): r = lax.ppermute(r, 'head', right)  45.6 us
    ppermute x9, waiting for transfers between devices, scatter_ring(): l = lax.ppermute(bl.astype(BF), 'head', left)  34.3 us
    all_gather x1, blocking collectives, body(): jax.lax.all_gather(frame_in, 'head')  33 us
    ppermute x9, waiting for transfers between devices, scatter_ring(): r = lax.ppermute(br.astype(BF), 'head', right)  31.9 us
    reduce_scatter x1, waiting for transfers between devices, body(): lax.psum_scatter(grad_out_w, 'fsdp', scatter_dimension=0, tiled=True)  30.4 us
  transfers between devices with their start and end apart: 78, of which 44 were waited for; matrix products, arithmetic and copies ran while one was open for 29% of the time, Pallas kernels for 0%

profile of v1, /device:TPU:0, one launch (start us, length us, event | category | flops | bytes accessed | tf_op | source)
XLA Modules:
  0.0 880.3 jit_solution(11524296791437319261)
XLA Ops:
  10.0 27.5 %all_to_all.40 = bf16[8,64,768]{2,1,0:T(8,128)(2,1)} all-to-all(bf16[8,64,768]{2,1,0:T(8,128)(2,1)S(1)} %reshape.375), channel_id=1, replica_groups=mesh['head'=8,'fsdp'=4] {'head'}, dimensions={0} | all-to-all | bytes 1572864 | tf_op jit(solution)/shard_map/all_to_all | solution.py:149
  45.0 53.5 %all-gather.1 = bf16[32,64,20]{1,2,0:T(8,128)(2,1)S(1)} all-gather(bf16[1,64,20]{1,2,0:T(8,128)(2,1)S(1)} %bitcast.498), channel_id=1, replica_groups=mesh['head'=8,'fsdp'=4] {'head','fsdp'}, dimensions={0}, use_global_device_ids=true | all-gather | bytes 84480 | tf_op jit(solution)/shard_map/all_gather | solution.py:142
  127.1 25.3 %collective-permute-done.33 = bf16[128,2048]{1,0:T(8,128)(2,1)} collective-permute-done((bf16[128,2048]{1,0:T(8,128)(2,1)S(1)}, bf16[128,2048]{1,0:T(8,128)(2,1)}, u32[]{:S(2)}, u32[]{:S(2)}) %collective-permute-start.33) | collective-permute-done | bytes 524320 | tf_op jit(solution)/shard_map/ppermute | solution.py:57
  157.2 7.3 collective-permute-done.3
  167.3 8.4 collective-permute-done.35
  179.5 7.4 collective-permute-done.5
  190.6 7.6 collective-permute-done.37
  208.3 5.3 fusion.10
  213.6 7.9 fusion.132
  221.7 33.0 %all-gather.2 = f32[8,2,1024]{2,1,0:T(2,128)} all-gather(f32[1,2,1024]{2,1,0:T(2,128)S(1)} %maximum_bitcast_fusion.4), channel_id=2, replica_groups=mesh['head'=8,'fsdp'=4] {'head'}, dimensions={0}, use_global_device_ids=true | all-gather | bytes 73728 | tf_op jit(solution)/shard_map/all_gather | solution.py:170
  271.3 11.0 %collective-permute-done.8 = bf16[1024,256]{0,1:T(8,128)(2,1)S(1)} collective-permute-done((bf16[1024,256]{0,1:T(8,128)(2,1)S(1)}, bf16[1024,256]{0,1:T(8,128)(2,1)S(1)}, u32[]{:S(2)}, u32[]{:S(2)}) %collective-permute-start.8) | collective-permute-done | bytes 524320 | tf_op jit(solution)/shard_map/ppermute | solution.py:56
  290.4 5.9 collective-permute-done.10
  300.8 5.9 collective-permute-done.12
  314.9 14.4 %multiply_reduce_fusion = (f32[1024]{0:T(1024)S(1)}, f32[1024,2048]{1,0:T(8,128)S(1)}) fusion(bf16[1024,2048]{0,1:T(8,128)(2,1)} %bitcast.39, bf16[2048,2048]{1,0:T(8,128)(2,1)} %all-gather.11.cloned.1.call-done, bf16[8,128,2048]{2,1,0:T(8,128)(2,1)} %fusion.75), kind=kOutput, calls=%fused_computation.30 | convolution fusion | flops 8598322176 | bytes 25169920 | tf_op jit(solution)/shard_map/dot_general | solution.py:103
  336.1 5.6 fusion.4
  341.8 10.0 %fusion.18 = f32[1024,1024]{1,0:T(8,128)} fusion(bf16[1024,2048]{1,0:T(8,128)(2,1)} %copy-done.6, bf16[2,2048,1024]{2,1,0:T(8,128)(2,1)} %all-gather.13.cloned.1.call-done), kind=kOutput, calls=%fused_computation.67 | convolution fusion | flops 4294967296 | bytes 12582912 | tf_op jit(solution)/shard_map/dot_general | solution.py:103
  351.8 6.3 fusion.23
  358.1 10.0 %fusion.20 = f32[1024,1024]{1,0:T(8,128)} fusion(bf16[1024,2048]{1,0:T(8,128)(2,1)} %copy-done.6, bf16[2,2048,1024]{2,1,0:T(8,128)(2,1)} %all-gather.15.cloned.1.call-done), kind=kOutput, calls=%fused_computation.69 | convolution fusion | flops 4294967296 | bytes 12582912 | tf_op jit(solution)/shard_map/dot_general | solution.py:103
  368.2 6.1 fusion.24
  374.3 12.2 %multiply_convert_fusion.5 = (bf16[1024,1024]{1,0:T(8,128)(2,1)S(1)}, bf16[1024,1024]{1,0:T(8,128)(2,1)S(1)}, bf16[1024,1024]{1,0:T(8,128)(2,1)}) fusion(f32[1024,1024]{1,0:T(8,128)} %fusion.18, f32[1024,1024]{1,0:T(8,128)} %fusion.20, bf16[1024,2048]{1,0:T(8,128)(2,1)} %bitcast.456, bf16[2,1024,2048]{2,1,0:T(8,128)(2,1)} %all-gather.17.cloned.1.call-done), kind=kOutput, calls=%fused_computation.49 | convolution fusion | flops 4310695936 | bytes 23068672 | tf_op jit(solution)/shard_map/dot_general | solution.py:103
  386.5 10.4 %fusion.17 = f32[1024,2048]{1,0:T(8,128)} fusion(bf16[1024,1024]{1,0:T(8,128)(2,1)S(1)} %get-tuple-element.89, bf16[2,2048,1024]{2,1,0:T(8,128)(2,1)} %all-gather.13.cloned.1.call-done), kind=kOutput, calls=%fused_computation.66 | convolution fusion | flops 4294967296 | bytes 14680064 | tf_op jit(solution)/shard_map/dot_general | solution.py:103
  397.0 9.1 %fusion.19 = f32[1024,2048]{1,0:T(8,128)} fusion(bf16[1024,1024]{1,0:T(8,128)(2,1)S(1)} %get-tuple-element.88, bf16[2,2048,1024]{2,1,0:T(8,128)(2,1)} %all-gather.15.cloned.1.call-done), kind=kOutput, calls=%fused_computation.68 | convolution fusion | flops 4294967296 | bytes 14680064 | tf_op jit(solution)/shard_map/dot_general | solution.py:103
  406.1 10.7 %multiply_convert_fusion.3 = (bf16[1024,1024]{1,0:T(8,128)(2,1)S(1)}, bf16[1024,1024]{1,0:T(8,128)(2,1)}, bf16[1024,1024]{1,0:T(8,128)(2,1)}) fusion(f32[1024,1024]{1,0:T(8,128)} %fusion.23, f32[1024,1024]{1,0:T(8,128)} %fusion.24, bf16[1024,2048]{1,0:T(8,128)(2,1)S(1)} %bitcast.455, bf16[2,1024,2048]{2,1,0:T(8,128)(2,1)S(1)} %bitcast.532), kind=kOutput, calls=%fused_computation.47 | convolution fusion | flops 4310695936 | bytes 23068672 | tf_op jit(solution)/shard_map/dot_general | solution.py:103
  416.8 9.1 %fusion.22 = f32[1024,2048]{1,0:T(8,128)} fusion(bf16[1024,1024]{1,0:T(8,128)(2,1)} %get-tuple-element.86, bf16[2,2048,1024]{2,1,0:T(8,128)(2,1)S(1)} %bitcast.534), kind=kOutput, calls=%fused_computation.71 | convolution fusion | flops 4294967296 | bytes 14680064 | tf_op jit(solution)/shard_map/dot_general | solution.py:103
  425.9 13.3 %add_convert_fusion = bf16[1024,2048]{1,0:T(8,128)(2,1)} fusion(f32[1024,2048]{1,0:T(8,128)} %fusion.22, f32[1024,2048]{1,0:T(8,128)} %fusion.17, f32[1024,2048]{1,0:T(8,128)} %fusion.19, bf16[1024,1024]{1,0:T(8,128)(2,1)S(1)} %get-tuple-element.85, bf16[2,2048,1024]{2,1,0:T(8,128)(2,1)} %all-gather.15.cloned.1.call-done), kind=kOutput, calls=%fused_computation.28 | convolution fusion | flops 4303355904 | bytes 35651584 | tf_op jit(solution)/shard_map/dot_general | solution.py:103
  442.6 5.2 collective-permute-done.40
  451.9 9.0 %collective-permute-done.41 = bf16[128,2048]{1,0:T(8,128)(2,1)S(1)} collective-permute-done((bf16[128,2048]{1,0:T(8,128)(2,1)S(1)}, bf16[128,2048]{1,0:T(8,128)(2,1)S(1)}, u32[]{:S(2)}, u32[]{:S(2)}) %collective-permute-start.41) | collective-permute-done | bytes 524320 | tf_op jit(solution)/shard_map/ppermute | solution.py:86
  463.7 7.5 convolution_convert_fusion.1
  474.7 12.6 %fusion.2 = (f32[1024]{0:T(1024)S(1)}, f32[1024]{0:T(1024)S(1)}, bf16[1024,2048]{1,0:T(8,128)(2,1)}, bf16[1024,2048]{1,0:T(8,128)(2,1)}, bf16[1024,2048]{1,0:T(8,128)(2,1)}) fusion(bf16[8,128,2048]{2,1,0:T(8,128)(2,1)} %fusion.77, bf16[1024,2048]{1,0:T(8,128)(2,1)S(1)} %convolution_convert_fusion.1, f32[1024]{0:T(1024)S(1)} %bitcast.502, ...), kind=kOutput, calls=%fused_computation.6 | convolution fusion | flops 4328519680 | bytes 27279360 | tf_op jit(solution)/shard_map/dot_general | solution.py:103
  487.8 3.6 all-to-all-start.1
  498.7 3.4 collective-permute-done.43
  511.7 6.5 convolution_convert_fusion.4
  519.0 4.5 all-to-all-start.2
  523.8 5.3 fusion.12
  529.1 4.8 all-to-all-done.2
  552.0 19.8 %psum.7 = f32[2,1024]{1,0:T(2,128)S(1)} all-reduce(f32[2,1024]{1,0:T(2,128)S(1)} %pad_maximum_fusion.17), channel_id=1, replica_groups=mesh['head'=8,'fsdp'=4] {'head'}, use_global_device_ids=true, to_apply=%region_23.24 | all-reduce | flops 2048 | bytes 16384 | tf_op jit(solution)/shard_map/psum | solution.py:285
  574.6 4.9 convolution_convert_fusion.3
  580.0 7.6 convert_bitcast_fusion.1
  587.6 6.2 convert_bitcast_fusion
  593.9 6.3 pad_maximum_fusion.2
  600.3 7.6 convert_bitcast_fusion.3
  607.9 6.3 convert_bitcast_fusion.2
  614.2 6.3 pad_maximum_fusion.1
  622.4 7.7 convert_bitcast_fusion.5
  630.1 6.2 convert_bitcast_fusion.4
  636.4 6.2 pad_maximum_fusion
  648.5 4.9 collective-permute-done.24
  656.8 5.7 collective-permute-done.56
  666.5 5.7 convolution_convert_fusion
  672.4 9.8 %collective-permute-done.58 = bf16[128,2048]{1,0:T(8,128)(2,1)S(1)} collective-permute-done((bf16[128,2048]{1,0:T(8,128)(2,1)S(1)}, bf16[128,2048]{1,0:T(8,128)(2,1)S(1)}, u32[]{:S(2)}, u32[]{:S(2)}) %collective-permute-start.58) | collective-permute-done | bytes 524320 | tf_op jit(solution)/shard_map/ppermute | solution.py:56
  688.9 7.3 collective-permute-done.60
  697.6 13.4 %collective-permute-done.49 = bf16[128,2048]{1,0:T(8,128)(2,1)S(1)} collective-permute-done((bf16[128,2048]{1,0:T(8,128)(2,1)S(1)}, bf16[128,2048]{1,0:T(8,128)(2,1)S(1)}, u32[]{:S(2)}, u32[]{:S(2)}) %collective-permute-start.49) | collective-permute-done | bytes 524320 | tf_op jit(solution)/shard_map/ppermute | solution.py:86
  711.2 5.5 collective-permute-done.62
  716.6 3.6 collective-permute-done.63
  732.8 4.2 collective-permute-done.54
  755.6 6.9 all-to-all-done.4
  762.5 3.5 all-to-all-start.3
  770.0 23.5 %collective-permute-done.31 = bf16[128,2048]{1,0:T(8,128)(2,1)S(1)} collective-permute-done((bf16[128,2048]{1,0:T(8,128)(2,1)S(1)}, bf16[128,2048]{1,0:T(8,128)(2,1)S(1)}, u32[]{:S(2)}, u32[]{:S(2)}) %collective-permute-start.31) | collective-permute-done | bytes 524320 | tf_op jit(solution)/shard_map/ppermute | solution.py:87
  793.5 4.2 fusion.45
  802.8 4.1 convert_element_type.606
  806.9 4.1 convert_element_type.601
  811.0 27.8 %reduce-scatter.10.cloned.1.call-done = bf16[2,512,1024]{2,1,0:T(8,128)(2,1)} async-done(((bf16[2,2048,1024]{2,1,0:T(8,128)(2,1)}), bf16[2,512,1024]{2,1,0:T(8,128)(2,1)}) %reduce-scatter.10.cloned.1.call-update) | async-done | bytes 2097168 | tf_op jit(solution)/shard_map/reduce_scatter | solution.py:235
  838.8 4.1 convert_element_type.598
  842.9 30.4 %reduce-scatter.8.cloned.1.call-done = f32[64,2048]{1,0:T(8,128)} async-done(((f32[256,2048]{1,0:T(8,128)}), f32[64,2048]{1,0:T(8,128)}) %reduce-scatter.8.cloned.1.call-update) | async-done | bytes 524304 | tf_op jit(solution)/shard_map/reduce_scatter | solution.py:304
  (496 shorter events, 224.0 us)
Async XLA Ops:
  7.2 206.4 %all-gather.9.cloned.1.call-start = ((), (), s32[]{:S(2)}) async-start(), calls=%async_computation.10 | async-start | bytes 3932160 | tf_op jit(solution)/shard_map/all_gather | solution.py:150
  37.5 277.4 %all-gather.11.cloned.1.call-start = ((), (), s32[]{:S(2)}) async-start(), calls=%async_computation.11 | async-start | bytes 8650752 | tf_op jit(solution)/shard_map/all_gather | solution.py:153
  38.2 303.5 %all-gather.13.cloned.1.call-start = ((), (), s32[]{:S(2)}) async-start(), calls=%async_computation.12 | async-start | bytes 10485760 | tf_op jit(solution)/shard_map/all_gather | solution.py:154
  39.0 319.1 %all-gather.15.cloned.1.call-start = ((), (), s32[]{:S(2)}) async-start(), calls=%async_computation.13 | async-start | bytes 10485760 | tf_op jit(solution)/shard_map/all_gather | solution.py:155
  39.5 334.8 %all-gather.17.cloned.1.call-start = ((), (), s32[]{:S(2)}) async-start(), calls=%async_computation.14 | async-start | bytes 10485760 | tf_op jit(solution)/shard_map/all_gather | solution.py:156
  39.6 69.0 %collective-permute-start.16 = (s32[128,16]{0,1:T(8,128)S(1)}, s32[128,16]{0,1:T(8,128)S(1)}, u32[]{:S(2)}, u32[]{:S(2)}) collective-permute-start(s32[128,16]{0,1:T(8,128)S(1)} %pad_add_fusion), channel_id=1, source_target_pairs={{0,8},{8,16},{16,24},{24,28},{28,20},{20,12},{12,4},{4,0},{1,9},{9... | collective-permute-start | bytes 24584 | tf_op jit(solution)/shard_map/ppermute | solution.py:56
  40.8 67.9 %collective-permute-start.17 = (s32[128,16]{0,1:T(8,128)S(1)}, s32[128,16]{0,1:T(8,128)S(1)}, u32[]{:S(2)}, u32[]{:S(2)}) collective-permute-start(s32[128,16]{0,1:T(8,128)S(1)} %pad_add_fusion), channel_id=1, source_target_pairs={{8,0},{16,8},{24,16},{28,24},{20,28},{12,20},{4,12},{0,4},{9,1},{1... | collective-permute-start | bytes 24584 | tf_op jit(solution)/shard_map/ppermute | solution.py:57
  41.7 80.4 %collective-permute-start = (bf16[128,2048]{1,0:T(8,128)(2,1)S(1)}, bf16[128,2048]{1,0:T(8,128)(2,1)S(1)}, u32[]{:S(2)}, u32[]{:S(2)}) collective-permute-start(bf16[128,2048]{1,0:T(8,128)(2,1)S(1)} %bitcast.422), channel_id=1, source_target_pairs={{0,8},{8,16},{16,24},{24,28},{28,20},{20,12},{12,4},{4,0},{1,9},{9... | collective-permute-start | bytes 1572872 | tf_op jit(solution)/shard_map/ppermute | solution.py:56
  42.8 80.6 %collective-permute-start.1 = (bf16[128,2048]{1,0:T(8,128)(2,1)S(1)}, bf16[128,2048]{1,0:T(8,128)(2,1)S(1)}, u32[]{:S(2)}, u32[]{:S(2)}) collective-permute-start(bf16[128,2048]{1,0:T(8,128)(2,1)S(1)} %bitcast.423), channel_id=1, source_target_pairs={{8,0},{16,8},{24,16},{28,24},{20,28},{12,20},{4,12},{0,4},{9,1},{1... | collective-permute-start | bytes 1572872 | tf_op jit(solution)/shard_map/ppermute | solution.py:57
  43.7 82.2 %collective-permute-start.32 = (bf16[128,2048]{1,0:T(8,128)(2,1)S(1)}, bf16[128,2048]{1,0:T(8,128)(2,1)S(1)}, u32[]{:S(2)}, u32[]{:S(2)}) collective-permute-start(bf16[128,2048]{1,0:T(8,128)(2,1)S(1)} %bitcast.436), channel_id=1, source_target_pairs={{0,8},{8,16},{16,24},{24,28},{28,20},{20,12},{12,4},{4,0},{1,9},{9... | collective-permute-start | bytes 1572872 | tf_op jit(solution)/shard_map/ppermute | solution.py:56
  120.3 32.1 %collective-permute-start.33 = (bf16[128,2048]{1,0:T(8,128)(2,1)S(1)}, bf16[128,2048]{1,0:T(8,128)(2,1)}, u32[]{:S(2)}, u32[]{:S(2)}) collective-permute-start(bf16[128,2048]{1,0:T(8,128)(2,1)S(1)} %bitcast.437), channel_id=1, source_target_pairs={{8,0},{16,8},{24,16},{28,24},{20,28},{12,20},{4,12},{0,4},{9,1},{1... | collective-permute-start | bytes 1572872 | tf_op jit(solution)/shard_map/ppermute | solution.py:57
  122.2 32.2 %collective-permute-start.2 = (bf16[128,2048]{1,0:T(8,128)(2,1)S(1)}, bf16[128,2048]{1,0:T(8,128)(2,1)S(1)}, u32[]{:S(2)}, u32[]{:S(2)}) collective-permute-start(bf16[128,2048]{1,0:T(8,128)(2,1)S(1)} %collective-permute-done), channel_id=1, source_target_pairs={{0,8},{8,16},{16,24},{24,28},{28,20},{20,12},{12,4},{4,0},{1,9},{9... | collective-permute-start | bytes 1572872 | tf_op jit(solution)/shard_map/ppermute | solution.py:56
  123.4 41.0 %collective-permute-start.3 = (bf16[128,2048]{1,0:T(8,128)(2,1)S(1)}, bf16[128,2048]{1,0:T(8,128)(2,1)S(1)}, u32[]{:S(2)}, u32[]{:S(2)}) collective-permute-start(bf16[128,2048]{1,0:T(8,128)(2,1)S(1)} %collective-permute-done.1), channel_id=1, source_target_pairs={{8,0},{16,8},{24,16},{28,24},{20,28},{12,20},{4,12},{0,4},{9,1},{1... | collective-permute-start | bytes 1572872 | tf_op jit(solution)/shard_map/ppermute | solution.py:57
  125.9 38.7 %collective-permute-start.34 = (bf16[128,2048]{1,0:T(8,128)(2,1)S(1)}, bf16[128,2048]{1,0:T(8,128)(2,1)S(1)}, u32[]{:S(2)}, u32[]{:S(2)}) collective-permute-start(bf16[128,2048]{1,0:T(8,128)(2,1)S(1)} %collective-permute-done.32), channel_id=1, source_target_pairs={{0,8},{8,16},{16,24},{24,28},{28,20},{20,12},{12,4},{4,0},{1,9},{9... | collective-permute-start | bytes 1572872 | tf_op jit(solution)/shard_map/ppermute | solution.py:56
  152.4 23.3 %collective-permute-start.35 = (bf16[128,2048]{1,0:T(8,128)(2,1)}, bf16[128,2048]{1,0:T(8,128)(2,1)S(1)}, u32[]{:S(2)}, u32[]{:S(2)}) collective-permute-start(bf16[128,2048]{1,0:T(8,128)(2,1)} %collective-permute-done.33), channel_id=1, source_target_pairs={{8,0},{16,8},{24,16},{28,24},{20,28},{12,20},{4,12},{0,4},{9,1},{1... | collective-permute-start | bytes 1572872 | tf_op jit(solution)/shard_map/ppermute | solution.py:57
  154.3 23.2 %collective-permute-start.4 = (bf16[128,2048]{1,0:T(8,128)(2,1)S(1)}, bf16[128,2048]{1,0:T(8,128)(2,1)S(1)}, u32[]{:S(2)}, u32[]{:S(2)}) collective-permute-start(bf16[128,2048]{1,0:T(8,128)(2,1)S(1)} %collective-permute-done.2), channel_id=1, source_target_pairs={{0,8},{8,16},{16,24},{24,28},{28,20},{20,12},{12,4},{4,0},{1,9},{9... | collective-permute-start | bytes 1572872 | tf_op jit(solution)/shard_map/ppermute | solution.py:56
  164.5 22.5 %collective-permute-start.5 = (bf16[128,2048]{1,0:T(8,128)(2,1)S(1)}, bf16[128,2048]{1,0:T(8,128)(2,1)S(1)}, u32[]{:S(2)}, u32[]{:S(2)}) collective-permute-start(bf16[128,2048]{1,0:T(8,128)(2,1)S(1)} %collective-permute-done.3), channel_id=1, source_target_pairs={{8,0},{16,8},{24,16},{28,24},{20,28},{12,20},{4,12},{0,4},{9,1},{1... | collective-permute-start | bytes 1572872 | tf_op jit(solution)/shard_map/ppermute | solution.py:57
  164.6 22.5 %collective-permute-start.36 = (bf16[128,2048]{1,0:T(8,128)(2,1)S(1)}, bf16[128,2048]{1,0:T(8,128)(2,1)S(1)}, u32[]{:S(2)}, u32[]{:S(2)}) collective-permute-start(bf16[128,2048]{1,0:T(8,128)(2,1)S(1)} %collective-permute-done.34), channel_id=1, source_target_pairs={{0,8},{8,16},{16,24},{24,28},{28,20},{20,12},{12,4},{4,0},{1,9},{9... | collective-permute-start | bytes 1572872 | tf_op jit(solution)/shard_map/ppermute | solution.py:56
  175.7 22.5 %collective-permute-start.37 = (bf16[128,2048]{1,0:T(8,128)(2,1)S(1)}, bf16[128,2048]{1,0:T(8,128)(2,1)S(1)}, u32[]{:S(2)}, u32[]{:S(2)}) collective-permute-start(bf16[128,2048]{1,0:T(8,128)(2,1)S(1)} %collective-permute-done.35), channel_id=1, source_target_pairs={{8,0},{16,8},{24,16},{28,24},{20,28},{12,20},{4,12},{0,4},{9,1},{1... | collective-permute-start | bytes 1572872 | tf_op jit(solution)/shard_map/ppermute | solution.py:57
  177.6 24.1 %collective-permute-start.6 = (bf16[64,2048]{1,0:T(8,128)(2,1)S(1)}, bf16[64,2048]{1,0:T(8,128)(2,1)S(1)}, u32[]{:S(2)}, u32[]{:S(2)}) collective-permute-start(bf16[64,2048]{1,0:T(8,128)(2,1)S(1)} %slice.410), channel_id=1, source_target_pairs={{0,8},{8,16},{16,24},{24,28},{28,20},{20,12},{12,4},{4,0},{1,9},{9... | collective-permute-start | bytes 786440 | tf_op jit(solution)/shard_map/ppermute | solution.py:60
  187.0 16.8 %collective-permute-start.7 = (bf16[64,2048]{1,0:T(8,128)(2,1)S(1)}, bf16[64,2048]{1,0:T(8,128)(2,1)S(1)}, u32[]{:S(2)}, u32[]{:S(2)}) collective-permute-start(bf16[64,2048]{1,0:T(8,128)(2,1)S(1)} %slice.411), channel_id=1, source_target_pairs={{8,0},{16,8},{24,16},{28,24},{20,28},{12,20},{4,12},{0,4},{9,1},{1... | collective-permute-start | bytes 786440 | tf_op jit(solution)/shard_map/ppermute | solution.py:61
  188.6 95.7 %collective-permute-start.38 = (bf16[64,2048]{1,0:T(8,128)(2,1)}, bf16[64,2048]{1,0:T(8,128)(2,1)}, u32[]{:S(2)}, u32[]{:S(2)}) collective-permute-start(bf16[64,2048]{1,0:T(8,128)(2,1)} %slice.443), channel_id=1, source_target_pairs={{0,8},{8,16},{16,24},{24,28},{28,20},{20,12},{12,4},{4,0},{1,9},{9... | collective-permute-start | bytes 786440 | tf_op jit(solution)/shard_map/ppermute | solution.py:60
  199.7 84.6 %collective-permute-start.39 = (bf16[64,2048]{1,0:T(8,128)(2,1)}, bf16[64,2048]{1,0:T(8,128)(2,1)}, u32[]{:S(2)}, u32[]{:S(2)}) collective-permute-start(bf16[64,2048]{1,0:T(8,128)(2,1)} %slice.444), channel_id=1, source_target_pairs={{8,0},{16,8},{24,16},{28,24},{20,28},{12,20},{4,12},{0,4},{9,1},{1... | collective-permute-start | bytes 786440 | tf_op jit(solution)/shard_map/ppermute | solution.py:61
  267.5 14.8 %collective-permute-start.8 = (bf16[1024,256]{0,1:T(8,128)(2,1)S(1)}, bf16[1024,256]{0,1:T(8,128)(2,1)S(1)}, u32[]{:S(2)}, u32[]{:S(2)}) collective-permute-start(bf16[1024,256]{0,1:T(8,128)(2,1)S(1)} %pad_maximum_fusion.8), channel_id=1, source_target_pairs={{0,8},{8,16},{16,24},{24,28},{28,20},{20,12},{12,4},{4,0},{1,9},{9... | collective-permute-start | bytes 1572872 | tf_op jit(solution)/shard_map/ppermute | solution.py:56
  267.6 14.8 %collective-permute-start.9 = (bf16[1024,256]{0,1:T(8,128)(2,1)S(1)}, bf16[1024,256]{0,1:T(8,128)(2,1)S(1)}, u32[]{:S(2)}, u32[]{:S(2)}) collective-permute-start(bf16[1024,256]{0,1:T(8,128)(2,1)S(1)} %pad_maximum_fusion.8), channel_id=1, source_target_pairs={{8,0},{16,8},{24,16},{28,24},{20,28},{12,20},{4,12},{0,4},{9,1},{1... | collective-permute-start | bytes 1572872 | tf_op jit(solution)/shard_map/ppermute | solution.py:57
  282.3 14.0 %collective-permute-start.10 = (bf16[1024,256]{0,1:T(8,128)(2,1)S(1)}, bf16[1024,256]{0,1:T(8,128)(2,1)S(1)}, u32[]{:S(2)}, u32[]{:S(2)}) collective-permute-start(bf16[1024,256]{0,1:T(8,128)(2,1)S(1)} %collective-permute-done.8), channel_id=1, source_target_pairs={{0,8},{8,16},{16,24},{24,28},{28,20},{20,12},{12,4},{4,0},{1,9},{9... | collective-permute-start | bytes 1572872 | tf_op jit(solution)/shard_map/ppermute | solution.py:56
  282.4 14.2 %collective-permute-start.11 = (bf16[1024,256]{0,1:T(8,128)(2,1)S(1)}, bf16[1024,256]{0,1:T(8,128)(2,1)S(1)}, u32[]{:S(2)}, u32[]{:S(2)}) collective-permute-start(bf16[1024,256]{0,1:T(8,128)(2,1)S(1)} %collective-permute-done.9), channel_id=1, source_target_pairs={{8,0},{16,8},{24,16},{28,24},{20,28},{12,20},{4,12},{0,4},{9,1},{1... | collective-permute-start | bytes 1572872 | tf_op jit(solution)/shard_map/ppermute | solution.py:57
  296.3 10.4 %collective-permute-start.12 = (bf16[1024,256]{0,1:T(8,128)(2,1)S(1)}, bf16[1024,256]{0,1:T(8,128)(2,1)S(1)}, u32[]{:S(2)}, u32[]{:S(2)}) collective-permute-start(bf16[1024,256]{0,1:T(8,128)(2,1)S(1)} %collective-permute-done.10), channel_id=1, source_target_pairs={{0,8},{8,16},{16,24},{24,28},{28,20},{20,12},{12,4},{4,0},{1,9},{9... | collective-permute-start | bytes 1572872 | tf_op jit(solution)/shard_map/ppermute | solution.py:56
  296.6 10.8 %collective-permute-start.13 = (bf16[1024,256]{0,1:T(8,128)(2,1)S(1)}, bf16[1024,256]{0,1:T(8,128)(2,1)S(1)}, u32[]{:S(2)}, u32[]{:S(2)}) collective-permute-start(bf16[1024,256]{0,1:T(8,128)(2,1)S(1)} %collective-permute-done.11), channel_id=1, source_target_pairs={{8,0},{16,8},{24,16},{28,24},{20,28},{12,20},{4,12},{0,4},{9,1},{1... | collective-permute-start | bytes 1572872 | tf_op jit(solution)/shard_map/ppermute | solution.py:57
  449.7 11.2 %collective-permute-start.41 = (bf16[128,2048]{1,0:T(8,128)(2,1)S(1)}, bf16[128,2048]{1,0:T(8,128)(2,1)S(1)}, u32[]{:S(2)}, u32[]{:S(2)}) collective-permute-start(bf16[128,2048]{1,0:T(8,128)(2,1)S(1)} %pad_maximum_fusion.11), channel_id=1, source_target_pairs={{0,8},{8,16},{16,24},{24,28},{28,20},{20,12},{12,4},{4,0},{1,9},{9... | collective-permute-start | bytes 1572872 | tf_op jit(solution)/shard_map/ppermute | solution.py:86
  450.4 20.8 %collective-permute-start.45 = (bf16[128,2048]{1,0:T(8,128)(2,1)S(1)}, bf16[128,2048]{1,0:T(8,128)(2,1)S(1)}, u32[]{:S(2)}, u32[]{:S(2)}) collective-permute-start(bf16[128,2048]{1,0:T(8,128)(2,1)S(1)} %pad_maximum_fusion.12), channel_id=1, source_target_pairs={{8,0},{16,8},{24,16},{28,24},{20,28},{12,20},{4,12},{0,4},{9,1},{1... | collective-permute-start | bytes 1572872 | tf_op jit(solution)/shard_map/ppermute | solution.py:87
  462.1 9.2 %collective-permute-start.42 = (bf16[128,2048]{1,0:T(8,128)(2,1)S(1)}, bf16[128,2048]{1,0:T(8,128)(2,1)S(1)}, u32[]{:S(2)}, u32[]{:S(2)}) collective-permute-start(bf16[128,2048]{1,0:T(8,128)(2,1)S(1)} %fusion.55), channel_id=1, source_target_pairs={{0,8},{8,16},{16,24},{24,28},{28,20},{20,12},{12,4},{4,0},{1,9},{9... | collective-permute-start | bytes 1572872 | tf_op jit(solution)/shard_map/ppermute | solution.py:86
  472.9 22.0 %collective-permute-start.46 = (bf16[128,2048]{1,0:T(8,128)(2,1)S(1)}, bf16[128,2048]{1,0:T(8,128)(2,1)S(1)}, u32[]{:S(2)}, u32[]{:S(2)}) collective-permute-start(bf16[128,2048]{1,0:T(8,128)(2,1)S(1)} %get-tuple-element.103), channel_id=1, source_target_pairs={{8,0},{16,8},{24,16},{28,24},{20,28},{12,20},{4,12},{0,4},{9,1},{1... | collective-permute-start | bytes 1572872 | tf_op jit(solution)/shard_map/ppermute | solution.py:87
  487.8 10.2 %all-to-all-start.1 = ((f32[8,2,128]{2,1,0:T(2,128)}), f32[8,2,128]{2,1,0:T(2,128)S(1)}, u32[]{:S(2)}, u32[]{:S(2)}) async-start(f32[8,2,128]{2,1,0:T(2,128)} %maximum_bitcast_fusion.5), calls=%async_computation.1 | async-start | bytes 16384 | tf_op jit(solution)/shard_map/all_to_all | solution.py:243
  492.8 9.2 %collective-permute-start.43 = (bf16[128,2048]{1,0:T(8,128)(2,1)S(1)}, bf16[128,2048]{1,0:T(8,128)(2,1)S(1)}, u32[]{:S(2)}, u32[]{:S(2)}) collective-permute-start(bf16[128,2048]{1,0:T(8,128)(2,1)S(1)} %get-tuple-element.102), channel_id=1, source_target_pairs={{0,8},{8,16},{16,24},{24,28},{28,20},{20,12},{12,4},{4,0},{1,9},{9... | collective-permute-start | bytes 1572872 | tf_op jit(solution)/shard_map/ppermute | solution.py:86
  496.0 9.2 %collective-permute-start.47 = (bf16[128,2048]{1,0:T(8,128)(2,1)S(1)}, bf16[128,2048]{1,0:T(8,128)(2,1)S(1)}, u32[]{:S(2)}, u32[]{:S(2)}) collective-permute-start(bf16[128,2048]{1,0:T(8,128)(2,1)S(1)} %fusion.54), channel_id=1, source_target_pairs={{8,0},{16,8},{24,16},{28,24},{20,28},{12,20},{4,12},{0,4},{9,1},{1... | collective-permute-start | bytes 1572872 | tf_op jit(solution)/shard_map/ppermute | solution.py:87
  519.0 14.8 %all-to-all-start.2 = ((bf16[128,8,256]{2,0,1:T(8,128)(2,1)}), bf16[128,8,256]{2,0,1:T(8,128)(2,1)S(1)}, u32[]{:S(2)}, u32[]{:S(2)}) async-start(bf16[128,8,256]{2,0,1:T(8,128)(2,1)} %bitcast.416), calls=%async_computation.2 | async-start | bytes 1048576 | tf_op jit(solution)/shard_map/all_to_all | solution.py:265
  523.5 239.0 %reduce-scatter.6.cloned.1.call-start = ((), (), s32[]{:S(2)}) async-start(), calls=%async_computation.15 | async-start | bytes 3932160 | tf_op jit(solution)/shard_map/reduce_scatter | solution.py:299
  579.5 223.3 %reduce-scatter.14.cloned.1.call-start = ((), (), s32[]{:S(2)}) async-start(), calls=%async_computation.19 | async-start | bytes 10485760 | tf_op jit(solution)/shard_map/reduce_scatter | solution.py:235
  600.2 206.7 %reduce-scatter.12.cloned.1.call-start = ((), (), s32[]{:S(2)}) async-start(), calls=%async_computation.18 | async-start | bytes 10485760 | tf_op jit(solution)/shard_map/reduce_scatter | solution.py:235
  620.5 218.2 %reduce-scatter.10.cloned.1.call-start = ((), (), s32[]{:S(2)}) async-start(), calls=%async_computation.17 | async-start | bytes 10485760 | tf_op jit(solution)/shard_map/reduce_scatter | solution.py:235
  642.6 230.6 %reduce-scatter.8.cloned.1.call-start = ((), (), s32[]{:S(2)}) async-start(), calls=%async_computation.16 | async-start | bytes 2621440 | tf_op jit(solution)/shard_map/reduce_scatter | solution.py:304
  644.1 9.3 %collective-permute-start.24 = (bf16[64,2048]{1,0:T(8,128)(2,1)S(1)}, bf16[64,2048]{1,0:T(8,128)(2,1)S(1)}, u32[]{:S(2)}, u32[]{:S(2)}) collective-permute-start(bf16[64,2048]{1,0:T(8,128)(2,1)S(1)} %get-tuple-element.116), channel_id=1, source_target_pairs={{0,8},{8,16},{16,24},{24,28},{28,20},{20,12},{12,4},{4,0},{1,9},{9... | collective-permute-start | bytes 786440 | tf_op jit(solution)/shard_map/ppermute | solution.py:75
  646.4 16.1 %collective-permute-start.56 = (bf16[128,2048]{1,0:T(8,128)(2,1)S(1)}, bf16[128,2048]{1,0:T(8,128)(2,1)S(1)}, u32[]{:S(2)}, u32[]{:S(2)}) collective-permute-start(bf16[128,2048]{1,0:T(8,128)(2,1)S(1)} %copy-done.37), channel_id=1, source_target_pairs={{0,8},{8,16},{16,24},{24,28},{28,20},{20,12},{12,4},{4,0},{1,9},{9... | collective-permute-start | bytes 1572872 | tf_op jit(solution)/shard_map/ppermute | solution.py:56
  646.5 17.5 %collective-permute-start.57 = (bf16[128,2048]{1,0:T(8,128)(2,1)S(1)}, bf16[128,2048]{1,0:T(8,128)(2,1)S(1)}, u32[]{:S(2)}, u32[]{:S(2)}) collective-permute-start(bf16[128,2048]{1,0:T(8,128)(2,1)S(1)} %copy-done.37), channel_id=1, source_target_pairs={{8,0},{16,8},{24,16},{28,24},{20,28},{12,20},{4,12},{0,4},{9,1},{1... | collective-permute-start | bytes 1572872 | tf_op jit(solution)/shard_map/ppermute | solution.py:57
  654.6 83.7 %collective-permute-start.29 = (bf16[128,2048]{1,0:T(8,128)(2,1)S(1)}, bf16[128,2048]{1,0:T(8,128)(2,1)}, u32[]{:S(2)}, u32[]{:S(2)}) collective-permute-start(bf16[128,2048]{1,0:T(8,128)(2,1)S(1)} %pad_maximum_fusion.10), channel_id=1, source_target_pairs={{8,0},{16,8},{24,16},{28,24},{20,28},{12,20},{4,12},{0,4},{9,1},{1... | collective-permute-start | bytes 1572872 | tf_op jit(solution)/shard_map/ppermute | solution.py:87
  656.5 71.4 %collective-permute-start.25 = (bf16[128,2048]{1,0:T(8,128)(2,1)S(1)}, bf16[128,2048]{1,0:T(8,128)(2,1)S(1)}, u32[]{:S(2)}, u32[]{:S(2)}) collective-permute-start(bf16[128,2048]{1,0:T(8,128)(2,1)S(1)} %pad_maximum_fusion.9), channel_id=1, source_target_pairs={{0,8},{8,16},{16,24},{24,28},{28,20},{20,12},{12,4},{4,0},{1,9},{9... | collective-permute-start | bytes 1572872 | tf_op jit(solution)/shard_map/ppermute | solution.py:86
  662.5 19.7 %collective-permute-start.58 = (bf16[128,2048]{1,0:T(8,128)(2,1)S(1)}, bf16[128,2048]{1,0:T(8,128)(2,1)S(1)}, u32[]{:S(2)}, u32[]{:S(2)}) collective-permute-start(bf16[128,2048]{1,0:T(8,128)(2,1)S(1)} %collective-permute-done.56), channel_id=1, source_target_pairs={{0,8},{8,16},{16,24},{24,28},{28,20},{20,12},{12,4},{4,0},{1,9},{9... | collective-permute-start | bytes 1572872 | tf_op jit(solution)/shard_map/ppermute | solution.py:56
  664.0 20.3 %collective-permute-start.59 = (bf16[128,2048]{1,0:T(8,128)(2,1)S(1)}, bf16[128,2048]{1,0:T(8,128)(2,1)S(1)}, u32[]{:S(2)}, u32[]{:S(2)}) collective-permute-start(bf16[128,2048]{1,0:T(8,128)(2,1)S(1)} %collective-permute-done.57), channel_id=1, source_target_pairs={{8,0},{16,8},{24,16},{28,24},{20,28},{12,20},{4,12},{0,4},{9,1},{1... | collective-permute-start | bytes 1572872 | tf_op jit(solution)/shard_map/ppermute | solution.py:57
  672.3 14.6 %collective-permute-start.48 = (bf16[64,2048]{1,0:T(8,128)(2,1)S(1)}, bf16[64,2048]{1,0:T(8,128)(2,1)S(1)}, u32[]{:S(2)}, u32[]{:S(2)}) collective-permute-start(bf16[64,2048]{1,0:T(8,128)(2,1)S(1)} %get-tuple-element.98), channel_id=1, source_target_pairs={{0,8},{8,16},{16,24},{24,28},{28,20},{20,12},{12,4},{4,0},{1,9},{9... | collective-permute-start | bytes 786440 | tf_op jit(solution)/shard_map/ppermute | solution.py:75
  684.3 11.9 %collective-permute-start.60 = (bf16[128,2048]{1,0:T(8,128)(2,1)S(1)}, bf16[128,2048]{1,0:T(8,128)(2,1)S(1)}, u32[]{:S(2)}, u32[]{:S(2)}) collective-permute-start(bf16[128,2048]{1,0:T(8,128)(2,1)S(1)} %collective-permute-done.58), channel_id=1, source_target_pairs={{0,8},{8,16},{16,24},{24,28},{28,20},{20,12},{12,4},{4,0},{1,9},{9... | collective-permute-start | bytes 1572872 | tf_op jit(solution)/shard_map/ppermute | solution.py:56
  687.0 9.6 %collective-permute-start.61 = (bf16[128,2048]{1,0:T(8,128)(2,1)S(1)}, bf16[128,2048]{1,0:T(8,128)(2,1)S(1)}, u32[]{:S(2)}, u32[]{:S(2)}) collective-permute-start(bf16[128,2048]{1,0:T(8,128)(2,1)S(1)} %collective-permute-done.59), channel_id=1, source_target_pairs={{8,0},{16,8},{24,16},{28,24},{20,28},{12,20},{4,12},{0,4},{9,1},{1... | collective-permute-start | bytes 1572872 | tf_op jit(solution)/shard_map/ppermute | solution.py:57
  688.7 34.3 %collective-permute-start.53 = (bf16[128,2048]{1,0:T(8,128)(2,1)S(1)}, bf16[128,2048]{1,0:T(8,128)(2,1)}, u32[]{:S(2)}, u32[]{:S(2)}) collective-permute-start(bf16[128,2048]{1,0:T(8,128)(2,1)S(1)} %pad_maximum_fusion.14), channel_id=1, source_target_pairs={{8,0},{16,8},{24,16},{28,24},{20,28},{12,20},{4,12},{0,4},{9,1},{1... | collective-permute-start | bytes 1572872 | tf_op jit(solution)/shard_map/ppermute | solution.py:87
  696.2 14.8 %collective-permute-start.49 = (bf16[128,2048]{1,0:T(8,128)(2,1)S(1)}, bf16[128,2048]{1,0:T(8,128)(2,1)S(1)}, u32[]{:S(2)}, u32[]{:S(2)}) collective-permute-start(bf16[128,2048]{1,0:T(8,128)(2,1)S(1)} %pad_maximum_fusion.13), channel_id=1, source_target_pairs={{0,8},{8,16},{16,24},{24,28},{28,20},{20,12},{12,4},{4,0},{1,9},{9... | collective-permute-start | bytes 1572872 | tf_op jit(solution)/shard_map/ppermute | solution.py:86
  696.6 20.0 %collective-permute-start.62 = (bf16[64,2048]{1,0:T(8,128)(2,1)S(1)}, bf16[64,2048]{1,0:T(8,128)(2,1)S(1)}, u32[]{:S(2)}, u32[]{:S(2)}) collective-permute-start(bf16[64,2048]{1,0:T(8,128)(2,1)S(1)} %slice.453), channel_id=1, source_target_pairs={{0,8},{8,16},{16,24},{24,28},{28,20},{20,12},{12,4},{4,0},{1,9},{9... | collective-permute-start | bytes 786440 | tf_op jit(solution)/shard_map/ppermute | solution.py:60
  711.0 9.2 %collective-permute-start.63 = (bf16[64,2048]{1,0:T(8,128)(2,1)S(1)}, bf16[64,2048]{1,0:T(8,128)(2,1)S(1)}, u32[]{:S(2)}, u32[]{:S(2)}) collective-permute-start(bf16[64,2048]{1,0:T(8,128)(2,1)S(1)} %slice.454), channel_id=1, source_target_pairs={{8,0},{16,8},{24,16},{28,24},{20,28},{12,20},{4,12},{0,4},{9,1},{1... | collective-permute-start | bytes 786440 | tf_op jit(solution)/shard_map/ppermute | solution.py:61
  716.6 9.3 %collective-permute-start.50 = (bf16[128,2048]{1,0:T(8,128)(2,1)S(1)}, bf16[128,2048]{1,0:T(8,128)(2,1)}, u32[]{:S(2)}, u32[]{:S(2)}) collective-permute-start(bf16[128,2048]{1,0:T(8,128)(2,1)S(1)} %fusion.50), channel_id=1, source_target_pairs={{0,8},{8,16},{16,24},{24,28},{28,20},{20,12},{12,4},{4,0},{1,9},{9... | collective-permute-start | bytes 1572872 | tf_op jit(solution)/shard_map/ppermute | solution.py:86
  729.1 9.4 %collective-permute-start.26 = (bf16[128,2048]{1,0:T(8,128)(2,1)S(1)}, bf16[128,2048]{1,0:T(8,128)(2,1)S(1)}, u32[]{:S(2)}, u32[]{:S(2)}) collective-permute-start(bf16[128,2048]{1,0:T(8,128)(2,1)S(1)} %fusion.61), channel_id=1, source_target_pairs={{0,8},{8,16},{16,24},{24,28},{28,20},{20,12},{12,4},{4,0},{1,9},{9... | collective-permute-start | bytes 1572872 | tf_op jit(solution)/shard_map/ppermute | solution.py:86
  732.8 11.4 %collective-permute-start.51 = (bf16[128,2048]{1,0:T(8,128)(2,1)S(1)}, bf16[128,2048]{1,0:T(8,128)(2,1)S(1)}, u32[]{:S(2)}, u32[]{:S(2)}) collective-permute-start(bf16[128,2048]{1,0:T(8,128)(2,1)S(1)} %get-tuple-element.94), channel_id=1, source_target_pairs={{0,8},{8,16},{16,24},{24,28},{28,20},{20,12},{12,4},{4,0},{1,9},{9... | collective-permute-start | bytes 1572872 | tf_op jit(solution)/shard_map/ppermute | solution.py:86
  741.3 24.8 %collective-permute-start.30 = (bf16[128,2048]{1,0:T(8,128)(2,1)}, bf16[128,2048]{1,0:T(8,128)(2,1)}, u32[]{:S(2)}, u32[]{:S(2)}) collective-permute-start(bf16[128,2048]{1,0:T(8,128)(2,1)} %get-tuple-element.113), channel_id=1, source_target_pairs={{8,0},{16,8},{24,16},{28,24},{20,28},{12,20},{4,12},{0,4},{9,1},{1... | collective-permute-start | bytes 1572872 | tf_op jit(solution)/shard_map/ppermute | solution.py:87
  751.3 11.2 %all-to-all-start.4 = ((f32[32,1,1280]{2,1,0:T(1,128)}), f32[32,1,1280]{2,1,0:T(1,128)S(1)}, u32[]{:S(2)}, u32[]{:S(2)}) async-start(f32[32,1,1280]{2,1,0:T(1,128)} %all_to_all.34), calls=%async_computation.6 | async-start | bytes 327680 | tf_op jit(solution)/shard_map/all_to_all | solution.py:321
  753.9 16.1 %collective-permute-start.27 = (bf16[128,2048]{1,0:T(8,128)(2,1)}, bf16[128,2048]{1,0:T(8,128)(2,1)}, u32[]{:S(2)}, u32[]{:S(2)}) collective-permute-start(bf16[128,2048]{1,0:T(8,128)(2,1)} %get-tuple-element.112), channel_id=1, source_target_pairs={{0,8},{8,16},{16,24},{24,28},{28,20},{20,12},{12,4},{4,0},{1,9},{9... | collective-permute-start | bytes 1572872 | tf_op jit(solution)/shard_map/ppermute | solution.py:86
  762.5 36.8 %all-to-all-start.3 = ((bf16[8,64,768]{2,1,0:T(8,128)(2,1)}), bf16[8,64,768]{2,1,0:T(8,128)(2,1)S(1)}, u32[]{:S(2)}, u32[]{:S(2)}) async-start(bf16[8,64,768]{2,1,0:T(8,128)(2,1)} %reduce-scatter.6.cloned.1.call-done), calls=%async_computation.4 | async-start | bytes 1572864 | tf_op jit(solution)/shard_map/all_to_all | solution.py:300
  767.4 26.1 %collective-permute-start.31 = (bf16[128,2048]{1,0:T(8,128)(2,1)S(1)}, bf16[128,2048]{1,0:T(8,128)(2,1)S(1)}, u32[]{:S(2)}, u32[]{:S(2)}) collective-permute-start(bf16[128,2048]{1,0:T(8,128)(2,1)S(1)} %fusion.60), channel_id=1, source_target_pairs={{8,0},{16,8},{24,16},{28,24},{20,28},{12,20},{4,12},{0,4},{9,1},{1... | collective-permute-start | bytes 1572872 | tf_op jit(solution)/shard_map/ppermute | solution.py:87
  (109 other events, 1604.6 us)
Sparse Core Ops, SparseCore 0:
  37.6 28.0 all-gather.8
  68.6 92.0 all-gather.10
  162.2 65.0 all-gather.12
  228.8 58.2 all-gather.14
  288.5 58.2 all-gather.16
  579.6 34.0 reduce-scatter.5
  616.4 71.6 reduce-scatter.13
  690.8 73.4 reduce-scatter.11
  767.0 71.7 reduce-scatter.9
  841.7 31.4 reduce-scatter.7
